TPU v7x, 32 devices: a whole 2x2x4 slice. The times are simulated.
32 devices in a mesh: band: 2 (over x), row: 16 (over z, y, core).
Axes of the slice: x: 2, y: 2, z: 4, core: 2. Of those that a mesh axis runs over, the one named last changes fastest.
Arguments:
- spectra: float32 [2, 16, 4096, 256], P(None, None, 'row', 'band'), parts along dimension 3, may hold values from -6 to 6
- coda_bins: int32 [8], P('band'), parts along dimension 0, may hold values from 0 to 15
- source_mask: int32 [128, 64], P('band'), parts along dimension 0, may hold values 0 or 1
Outputs:
- third_order: float32 [8192, 2, 4, 128], P(('band', 'row')), parts along dimension 0
There are 2 independent parts, one for each index of `band`. A program takes and returns all parts, laid end to end along the dimension named above; each array names one. Nothing has to cross between parts.
Inputs may be any that keep to these rules, and one draw needn't show every extreme that they name: `coda_bins`: each entry is a bin of the band's spectrum; entries may repeat.
All inputs are finite; a program needn't handle non-finite values.
Results may differ from a plain program's by a relative error of at most 0.004.
Values may be sent and summed in bfloat16 or wider, within the bound.
No kernel may reach another device: no remote copies, remote signals or barrier semaphores. Data moves between devices by JAX's collectives and lax.ppermute only.
A program may use at most 128 MiB of HBM per device.

v0:
```python
import functools

import jax
import jax.numpy as jnp
from jax import lax
from jax.experimental import pallas as pl
from jax.experimental.pallas import tpu as pltpu
from jax.sharding import PartitionSpec as P

NTGT = 128
NT_DIMS = (((1,), (1,)), ((), ()))


def whiten_kernel(bins, spectra, *refs):
    count = (len(refs) - 2) // 1
    outs, held, sems = refs[:count], refs[count], refs[count + 1]
    copies = [
        pltpu.make_async_copy(spectra.at[:, bins[slot]], held.at[slot], sems.at[slot])
        for slot in range(count)
    ]
    for copy in copies:
        copy.start()
    for slot in range(count):
        copies[slot].wait()
        real, imag = held[slot, 0], held[slot, 1]
        power = jnp.mean(real * real + imag * imag, axis=1, keepdims=True)
        scale = 1.0 / jnp.sqrt(power + 1e-06)
        outs[slot][...] = jnp.concatenate([real * scale, imag * scale], axis=1).astype(jnp.bfloat16)


def whiten(spectra, bins):
    _, _, own, windows = spectra.shape
    count = bins.shape[0]
    return pl.pallas_call(
        whiten_kernel,
        grid_spec=pltpu.PrefetchScalarGridSpec(
            num_scalar_prefetch=1,
            grid=(1,),
            in_specs=[pl.BlockSpec(memory_space=pl.ANY)],
            out_specs=[pl.BlockSpec((own, 2 * windows), lambda s, b: (0, 0))] * count,
            scratch_shapes=[
                pltpu.VMEM((count, 2, own, windows), jnp.float32),
                pltpu.SemaphoreType.DMA((count,)),
            ],
        ),
        out_shape=[jax.ShapeDtypeStruct((own, 2 * windows), jnp.bfloat16)] * count,
        name="whiten",
    )(bins, spectra)


def quarter_turn(rows):
    half = rows.shape[1] // 2
    return jnp.concatenate([rows[:, half:], -rows[:, :half]], axis=1)


def third_kernel(layout, *refs):
    count, spread, own, spacing, grp = layout
    blocks = refs[: count * spread]
    kid, igrp, mask = refs[count * spread : count * spread + 3]
    outs = refs[count * spread + 3 : count * spread + 3 + count]
    everyone, turned, tmask, targets, acc = refs[count * spread + 3 + count :]
    f32, bf16 = jnp.float32, jnp.bfloat16
    chunk = spread * own
    groups = mask.shape[0]
    for at in range(count * spread):
        everyone[pl.ds(at * own, own), :] = blocks[at][...]
    for slot in range(count):
        turned[pl.ds(slot * own, own), :] = quarter_turn(blocks[slot * spread][...])
    table = mask[...].astype(f32).astype(bf16)
    tgroup = (lax.broadcasted_iota(jnp.int32, (groups, 2 * NTGT), 1) % NTGT) * spacing // grp
    lanes = (tgroup == lax.broadcasted_iota(jnp.int32, tgroup.shape, 0)).astype(f32).astype(bf16)
    tmask[...] = lax.dot_general(table, lanes, (((0,), (0,)), ((), ())), preferred_element_type=f32)
    rowpick = (igrp[...] == lax.broadcasted_iota(jnp.int32, (igrp.shape[0], groups), 1)).astype(f32).astype(bf16)
    rowmask = jnp.dot(rowpick, table, preferred_element_type=f32).astype(bf16)

    def pick(step, total):
        start = pl.multiple_of(step * chunk, chunk)
        ids = kid[pl.ds(step, 1), :]
        wanted = lax.broadcasted_iota(jnp.int32, (NTGT, chunk), 0) * spacing
        onehot = (ids == wanted).astype(f32).astype(bf16)
        return total + jnp.dot(onehot, everyone[pl.ds(start, chunk), :], preferred_element_type=f32)

    tgt = lax.fori_loop(0, count, pick, jnp.zeros((NTGT, everyone.shape[1]), f32)).astype(bf16)
    tturn = quarter_turn(tgt)
    targets[0] = jnp.concatenate([tgt, -tturn], axis=0)
    targets[1] = jnp.concatenate([tturn, tgt], axis=0)
    acc[...] = jnp.zeros_like(acc)

    def step_body(step, carry):
        start = pl.multiple_of(step * chunk, chunk)
        right = everyone[pl.ds(start, chunk), :]
        ids = kid[pl.ds(step, 1), :]
        colpick = (
            lax.broadcasted_iota(jnp.int32, (groups, chunk), 0) == ids // grp
        ).astype(f32)
        rows = jnp.dot(rowpick_mask(), colpick.astype(bf16), preferred_element_type=f32)
        tm = lax.dot_general(
            colpick.astype(bf16), tmask[...].astype(bf16), (((0,), (0,)), ((), ())), preferred_element_type=f32
        )
        r1 = (lax.dot_general(right, targets[0], NT_DIMS, preferred_element_type=f32) * tm).astype(bf16)
        r2 = (lax.dot_general(right, targets[1], NT_DIMS, preferred_element_type=f32) * tm).astype(bf16)
        for slot in range(count):
            at = pl.ds(slot * own, own)
            per = own // grp
            weight = jnp.broadcast_to(
                rows[slot * per : (slot + 1) * per][:, None, :], (per, grp, chunk)
            ).reshape(own, chunk)
            left = blocks[slot * spread][...]
            real = (lax.dot_general(left, right, NT_DIMS, preferred_element_type=f32) * weight).astype(bf16)
            imag = (lax.dot_general(turned[at, :], right, NT_DIMS, preferred_element_type=f32) * weight).astype(bf16)
            acc[at, :] += jnp.dot(real, r1, preferred_element_type=f32) + jnp.dot(
                imag, r2, preferred_element_type=f32
            )
        return carry

    def rowpick_mask():
        return rowmask

    lax.fori_loop(0, count, step_body, 0)
    windows = everyone.shape[1] // 2
    for slot in range(count):
        outs[slot][...] = (acc[pl.ds(slot * own, own), :] * (1.0 / (windows * windows))).astype(bf16)


def third(blocks, kid, igrp, mask, layout):
    count, spread, own, spacing, grp = layout
    width = blocks[0].shape[1]
    f32, bf16 = jnp.float32, jnp.bfloat16
    vmem = pl.BlockSpec(memory_space=pltpu.VMEM)
    return pl.pallas_call(
        functools.partial(third_kernel, layout),
        in_specs=[vmem] * (len(blocks) + 3),
        out_specs=[vmem] * count,
        out_shape=[jax.ShapeDtypeStruct((own, 2 * NTGT), bf16)] * count,
        scratch_shapes=[
            pltpu.VMEM((count * spread * own, width), bf16),
            pltpu.VMEM((count * own, width), bf16),
            pltpu.VMEM((mask.shape[0], 2 * NTGT), f32),
            pltpu.VMEM((2, 2 * NTGT, width), bf16),
            pltpu.VMEM((count * own, 2 * NTGT), f32),
        ],
        name="third",
    )(*blocks, kid, igrp, mask)


def finish_kernel(place, *refs):
    blocks, out = refs[:-1], refs[-1]
    count = len(blocks)
    own = blocks[0].shape[0]
    for slot, block in enumerate(blocks):
        value = block[...].astype(jnp.float32)
        for part in range(2):
            out[pl.ds(part * count + place[slot], own, stride=2 * count), :] = value[
                :, part * NTGT : (part + 1) * NTGT
            ]


def finish(blocks, place):
    own = blocks[0].shape[0]
    count = len(blocks)
    vmem = pl.BlockSpec(memory_space=pltpu.VMEM)
    out = pl.pallas_call(
        finish_kernel,
        in_specs=[pl.BlockSpec(memory_space=pltpu.SMEM)] + [vmem] * count,
        out_specs=vmem,
        out_shape=jax.ShapeDtypeStruct((own * 2 * count, NTGT), jnp.float32),
        name="finish",
    )(place, *blocks)
    return out.reshape(own, 2, count, NTGT)


def on_device(rows, spectra, coda_bins, source_mask):
    count = coda_bins.shape[0]
    spread = rows // count
    own = spectra.shape[2]
    channels = own * rows
    spacing = channels // NTGT
    grp = channels // source_mask.shape[0]
    me = lax.axis_index("row").astype(jnp.int32)
    mine, seat = me // spread, me % spread

    def swap(value, bits):
        return lax.ppermute(value, "row", [(r, r ^ bits) for r in range(rows)])

    slots = jnp.arange(count, dtype=jnp.int32)
    place = mine ^ slots
    white = whiten(spectra, coda_bins[place])
    blocks = [[white[0]] + [None] * (spread - 1)]
    for slot in range(1, count):
        blocks.append([swap(white[slot], slot * spread)] + [None] * (spread - 1))
    bit = spread // 2
    while bit >= 1:
        for slot in range(count):
            for held in range(0, spread, 2 * bit):
                blocks[slot][held + bit] = swap(blocks[slot][held], bit)
        bit //= 2
    seats = seat ^ jnp.arange(spread, dtype=jnp.int32)
    source = place[:, None] * spread + seats[None, :]
    kid = (source[:, :, None] * own + jnp.arange(own, dtype=jnp.int32)).reshape(count, spread * own)
    per = own // grp
    igrp = (((place * spread + seat) * per)[:, None] + jnp.arange(per, dtype=jnp.int32)).reshape(-1, 1)
    flat = [blocks[slot][held] for slot in range(count) for held in range(spread)]
    parts = third(flat, kid, igrp, source_mask, (count, spread, own, spacing, grp))
    back = [parts[0]] + [swap(parts[slot], slot * spread) for slot in range(1, count)]
    return finish(back, place)


def solution(mesh):
    return jax.shard_map(
        functools.partial(on_device, mesh.shape["row"]),
        mesh=mesh,
        in_specs=(P(None, None, "row", "band"), P("band"), P("band", None)),
        out_specs=P(("band", "row"), None, None, None),
        check_vma=False,
    )
```

profile of v0, /device:TPU:0, one launch (start us, length us, event | category | flops | bytes accessed | tf_op | source)
XLA Modules:
  0.0 68.0 jit_solution(11410147695282013912)
XLA Ops:
  0.0 0.6 copy-done
  0.7 1.2 %gather_fusion = s32[4]{0:T(128)} fusion(s32[4]{0:T(128)S(1)} %copy-done, s32[1024]{0:T(1024)S(1)} %pad_clamp_fusion), kind=kCustom, calls=%fused_computation | custom fusion | bytes 48 | tf_op jit(solution)/shard_map/gather | solution.py:187
  1.8 2.9 %whiten.1 = (bf16[256,256]{1,0:T(8,128)(2,1)}, bf16[256,256]{1,0:T(8,128)(2,1)}, bf16[256,256]{1,0:T(8,128)(2,1)}, bf16[256,256]{1,0:T(8,128)(2,1)}) custom-call(s32[4]{0:T(128)} %gather_fusion, f32[2,16,256,128]{3,2,1,0:T(8,128)} %spectra.1), custom_call_target="tpu_custom_call" | custom-call | tf_op jit(solution)/shard_map/whiten/pallas_call | solution.py:34
  4.7 3.1 %collective-permute-start.1 = (bf16[256,256]{1,0:T(8,128)(2,1)}, bf16[256,256]{1,0:T(8,128)(2,1)S(1)}, u32[]{:S(2)}, u32[]{:S(2)}) collective-permute-start(bf16[256,256]{1,0:T(8,128)(2,1)} %get-tuple-element.13.refs_0_), channel_id=1, source_target_pairs={{0,2},{1,3},{2,0},{3,1},{4,6},{5,7},{6,4},{7,5},{8,10},{9,11},{10,... | collective-permute-start | bytes 393224 | tf_op jit(solution)/shard_map/ppermute | solution.py:183
  7.8 0.0 collective-permute-start
  7.8 1.6 %collective-permute-start.3 = (bf16[256,256]{1,0:T(8,128)(2,1)}, bf16[256,256]{1,0:T(8,128)(2,1)S(1)}, u32[]{:S(2)}, u32[]{:S(2)}) collective-permute-start(bf16[256,256]{1,0:T(8,128)(2,1)} %get-tuple-element.14), channel_id=1, source_target_pairs={{0,4},{1,5},{2,6},{3,7},{4,0},{5,1},{6,2},{7,3},{8,12},{9,13},{10,... | collective-permute-start | bytes 393224 | tf_op jit(solution)/shard_map/ppermute | solution.py:183
  9.4 2.6 %collective-permute-start.7 = (bf16[256,256]{1,0:T(8,128)(2,1)}, bf16[256,256]{1,0:T(8,128)(2,1)S(1)}, u32[]{:S(2)}, u32[]{:S(2)}) collective-permute-start(bf16[256,256]{1,0:T(8,128)(2,1)} %get-tuple-element.15), channel_id=1, source_target_pairs={{0,8},{1,9},{2,10},{3,11},{4,12},{5,13},{6,14},{7,15},{8,0},{9,1},... | collective-permute-start | bytes 393224 | tf_op jit(solution)/shard_map/ppermute | solution.py:183
  11.9 0.2 collective-permute-start.11
  12.2 0.1 iota_add_fusion
  12.3 0.7 add.99.refs_17_
  12.9 0.1 add_multiply_fusion
  13.0 3.2 %collective-permute-done.3.refs_4_ = bf16[256,256]{1,0:T(8,128)(2,1)S(1)} collective-permute-done((bf16[256,256]{1,0:T(8,128)(2,1)}, bf16[256,256]{1,0:T(8,128)(2,1)S(1)}, u32[]{:S(2)}, u32[]{:S(2)}) %collective-permute-start.3) | collective-permute-done | bytes 131104 | tf_op jit(solution)/shard_map/ppermute | solution.py:183
  16.2 0.3 collective-permute-start.5
  16.5 6.0 %collective-permute-done.7.refs_8_ = bf16[256,256]{1,0:T(8,128)(2,1)S(1)} collective-permute-done((bf16[256,256]{1,0:T(8,128)(2,1)}, bf16[256,256]{1,0:T(8,128)(2,1)S(1)}, u32[]{:S(2)}, u32[]{:S(2)}) %collective-permute-start.7) | collective-permute-done | bytes 131104 | tf_op jit(solution)/shard_map/ppermute | solution.py:183
  22.5 0.0 collective-permute-start.4
  22.5 0.0 collective-permute-done.11.refs_12_
  22.5 0.6 collective-permute-start.9
  23.1 0.0 collective-permute-done.1.refs_2_
  23.1 0.2 collective-permute-start.8
  23.2 0.0 collective-permute-done.refs_1_
  23.3 1.5 %collective-permute-start.13 = (bf16[256,256]{1,0:T(8,128)(2,1)S(1)}, bf16[256,256]{1,0:T(8,128)(2,1)S(1)}, u32[]{:S(2)}, u32[]{:S(2)}) collective-permute-start(bf16[256,256]{1,0:T(8,128)(2,1)S(1)} %collective-permute-done.11.refs_12_), channel_id=1, source_target_pairs={{0,2},{1,3},{2,0},{3,1},{4,6},{5,7},{6,4},{7,5},{8,10},{9,11},{10,... | collective-permute-start | bytes 393224 | tf_op jit(solution)/shard_map/ppermute | solution.py:183
  24.8 0.1 broadcast_bitcast_fusion
  24.9 0.0 collective-permute-done.5.refs_6_
  24.9 0.1 collective-permute-start.12
  25.0 0.0 collective-permute-done.4.refs_5_
  25.0 0.4 collective-permute-start.2
  25.4 3.5 %collective-permute-done.9.refs_10_ = bf16[256,256]{1,0:T(8,128)(2,1)S(1)} collective-permute-done((bf16[256,256]{1,0:T(8,128)(2,1)S(1)}, bf16[256,256]{1,0:T(8,128)(2,1)S(1)}, u32[]{:S(2)}, u32[]{:S(2)}) %collective-permute-start.9) | collective-permute-done | bytes 131104 | tf_op jit(solution)/shard_map/ppermute | solution.py:183
  29.0 0.0 collective-permute-done.8.refs_9_
  29.0 0.5 collective-permute-start.10
  29.5 1.8 %collective-permute-done.13.refs_14_ = bf16[256,256]{1,0:T(8,128)(2,1)S(1)} collective-permute-done((bf16[256,256]{1,0:T(8,128)(2,1)S(1)}, bf16[256,256]{1,0:T(8,128)(2,1)S(1)}, u32[]{:S(2)}, u32[]{:S(2)}) %collective-permute-start.13) | collective-permute-done | bytes 131104 | tf_op jit(solution)/shard_map/ppermute | solution.py:183
  31.2 0.0 collective-permute-start.14
  31.2 0.7 broadcast_add_fusion.refs_16_
  31.9 0.0 collective-permute-done.2.refs_3_
  31.9 0.0 collective-permute-done.6.refs_7_
  32.0 0.6 collective-permute-done.14.refs_15_
  32.7 0.0 copy-done.14
  32.7 0.6 copy-done.15
  33.4 16.7 %third.1 = (bf16[256,256]{1,0:T(8,128)(2,1)}, bf16[256,256]{1,0:T(8,128)(2,1)}, bf16[256,256]{1,0:T(8,128)(2,1)}, bf16[256,256]{1,0:T(8,128)(2,1)}) custom-call(bf16[256,256]{1,0:T(8,128)(2,1)} %get-tuple-element.13.refs_0_, bf16[256,256]{1,0:T(8,128)(2,1)} %copy-done.2, bf16[256,256]{1,0:T(8,128)(2,1)} %copy-done.1, bf16[256,256]{1,0:T(8,128)(2,1)} %copy-done.12, ...), custom_call_target="tpu_custom_call" | custom-call | tf_op jit(solution)/shard_map/third/pallas_call | solution.py:130
  50.1 1.7 %collective-permute-start.15 = (bf16[256,256]{1,0:T(8,128)(2,1)}, bf16[256,256]{1,0:T(8,128)(2,1)S(1)}, u32[]{:S(2)}, u32[]{:S(2)}) collective-permute-start(bf16[256,256]{1,0:T(8,128)(2,1)} %get-tuple-element.18), channel_id=1, source_target_pairs={{0,4},{1,5},{2,6},{3,7},{4,0},{5,1},{6,2},{7,3},{8,12},{9,13},{10,... | collective-permute-start | bytes 393224 | tf_op jit(solution)/shard_map/ppermute | solution.py:183
  51.8 1.4 %collective-permute-start.16 = (bf16[256,256]{1,0:T(8,128)(2,1)}, bf16[256,256]{1,0:T(8,128)(2,1)S(1)}, u32[]{:S(2)}, u32[]{:S(2)}) collective-permute-start(bf16[256,256]{1,0:T(8,128)(2,1)} %get-tuple-element.19), channel_id=1, source_target_pairs={{0,8},{1,9},{2,10},{3,11},{4,12},{5,13},{6,14},{7,15},{8,0},{9,1},... | collective-permute-start | bytes 393224 | tf_op jit(solution)/shard_map/ppermute | solution.py:183
  53.1 1.3 %collective-permute-start.17 = (bf16[256,256]{1,0:T(8,128)(2,1)}, bf16[256,256]{1,0:T(8,128)(2,1)S(1)}, u32[]{:S(2)}, u32[]{:S(2)}) collective-permute-start(bf16[256,256]{1,0:T(8,128)(2,1)} %get-tuple-element.20), channel_id=1, source_target_pairs={{0,12},{1,13},{2,14},{3,15},{4,8},{5,9},{6,10},{7,11},{8,4},{9,5},... | collective-permute-start | bytes 393224 | tf_op jit(solution)/shard_map/ppermute | solution.py:183
  54.5 0.6 iota_xor_fusion.1.place
  55.1 3.3 %collective-permute-done.15.refs_1_ = bf16[256,256]{1,0:T(8,128)(2,1)S(1)} collective-permute-done((bf16[256,256]{1,0:T(8,128)(2,1)}, bf16[256,256]{1,0:T(8,128)(2,1)S(1)}, u32[]{:S(2)}, u32[]{:S(2)}) %collective-permute-start.15) | collective-permute-done | bytes 131104 | tf_op jit(solution)/shard_map/ppermute | solution.py:183
  58.4 6.6 %collective-permute-done.16.refs_2_ = bf16[256,256]{1,0:T(8,128)(2,1)S(1)} collective-permute-done((bf16[256,256]{1,0:T(8,128)(2,1)}, bf16[256,256]{1,0:T(8,128)(2,1)S(1)}, u32[]{:S(2)}, u32[]{:S(2)}) %collective-permute-start.16) | collective-permute-done | bytes 131104 | tf_op jit(solution)/shard_map/ppermute | solution.py:183
  64.9 0.0 collective-permute-done.17.refs_3_
  64.9 0.6 copy-done.17
  65.6 0.1 copy-done.18
  65.6 2.3 %finish.1 = f32[2048,128]{1,0:T(8,128)} custom-call(s32[4]{0:T(128)} %iota_xor_fusion.1.place, bf16[256,256]{1,0:T(8,128)(2,1)} %get-tuple-element.17.refs_0_, bf16[256,256]{1,0:T(8,128)(2,1)} %copy-done.16, bf16[256,256]{1,0:T(8,128)(2,1)} %copy-done.17, bf16[256,256]{1,0:T(8,128)(2,1)} %copy-done.18), custom_call_target="tpu_custom_call" | custom-call | tf_op jit(solution)/shard_map/finish/pallas_call | solution.py:162
  (43 shorter events, 0.1 us)
Async XLA Ops:
  0.0 0.7 copy-start
  4.7 18.4 %collective-permute-start.1 = (bf16[256,256]{1,0:T(8,128)(2,1)}, bf16[256,256]{1,0:T(8,128)(2,1)S(1)}, u32[]{:S(2)}, u32[]{:S(2)}) collective-permute-start(bf16[256,256]{1,0:T(8,128)(2,1)} %get-tuple-element.13.refs_0_), channel_id=1, source_target_pairs={{0,2},{1,3},{2,0},{3,1},{4,6},{5,7},{6,4},{7,5},{8,10},{9,11},{10,... | collective-permute-start | bytes 393224 | tf_op jit(solution)/shard_map/ppermute | solution.py:183
  7.8 15.5 %collective-permute-start = (bf16[256,256]{1,0:T(8,128)(2,1)}, bf16[256,256]{1,0:T(8,128)(2,1)S(1)}, u32[]{:S(2)}, u32[]{:S(2)}) collective-permute-start(bf16[256,256]{1,0:T(8,128)(2,1)} %get-tuple-element.13.refs_0_), channel_id=1, source_target_pairs={{0,1},{1,0},{2,3},{3,2},{4,5},{5,4},{6,7},{7,6},{8,9},{9,8},{10,11... | collective-permute-start | bytes 393224 | tf_op jit(solution)/shard_map/ppermute | solution.py:183
  7.8 8.4 %collective-permute-start.3 = (bf16[256,256]{1,0:T(8,128)(2,1)}, bf16[256,256]{1,0:T(8,128)(2,1)S(1)}, u32[]{:S(2)}, u32[]{:S(2)}) collective-permute-start(bf16[256,256]{1,0:T(8,128)(2,1)} %get-tuple-element.14), channel_id=1, source_target_pairs={{0,4},{1,5},{2,6},{3,7},{4,0},{5,1},{6,2},{7,3},{8,12},{9,13},{10,... | collective-permute-start | bytes 393224 | tf_op jit(solution)/shard_map/ppermute | solution.py:183
  9.4 13.1 %collective-permute-start.7 = (bf16[256,256]{1,0:T(8,128)(2,1)}, bf16[256,256]{1,0:T(8,128)(2,1)S(1)}, u32[]{:S(2)}, u32[]{:S(2)}) collective-permute-start(bf16[256,256]{1,0:T(8,128)(2,1)} %get-tuple-element.15), channel_id=1, source_target_pairs={{0,8},{1,9},{2,10},{3,11},{4,12},{5,13},{6,14},{7,15},{8,0},{9,1},... | collective-permute-start | bytes 393224 | tf_op jit(solution)/shard_map/ppermute | solution.py:183
  11.9 10.6 %collective-permute-start.11 = (bf16[256,256]{1,0:T(8,128)(2,1)}, bf16[256,256]{1,0:T(8,128)(2,1)S(1)}, u32[]{:S(2)}, u32[]{:S(2)}) collective-permute-start(bf16[256,256]{1,0:T(8,128)(2,1)} %get-tuple-element.16), channel_id=1, source_target_pairs={{0,12},{1,13},{2,14},{3,15},{4,8},{5,9},{6,10},{7,11},{8,4},{9,5},... | collective-permute-start | bytes 393224 | tf_op jit(solution)/shard_map/ppermute | solution.py:183
  16.2 16.4 %copy-start.3 = (bf16[256,256]{1,0:T(8,128)(2,1)}, bf16[256,256]{1,0:T(8,128)(2,1)S(1)}, u32[]{:S(2)}) copy-start(bf16[256,256]{1,0:T(8,128)(2,1)S(1)} %collective-permute-done.3.refs_4_) | copy-start | bytes 393220
  16.2 8.7 %collective-permute-start.5 = (bf16[256,256]{1,0:T(8,128)(2,1)S(1)}, bf16[256,256]{1,0:T(8,128)(2,1)S(1)}, u32[]{:S(2)}, u32[]{:S(2)}) collective-permute-start(bf16[256,256]{1,0:T(8,128)(2,1)S(1)} %collective-permute-done.3.refs_4_), channel_id=1, source_target_pairs={{0,2},{1,3},{2,0},{3,1},{4,6},{5,7},{6,4},{7,5},{8,10},{9,11},{10,... | collective-permute-start | bytes 393224 | tf_op jit(solution)/shard_map/ppermute | solution.py:183
  22.5 10.1 %copy-start.4 = (bf16[256,256]{1,0:T(8,128)(2,1)}, bf16[256,256]{1,0:T(8,128)(2,1)S(1)}, u32[]{:S(2)}) copy-start(bf16[256,256]{1,0:T(8,128)(2,1)S(1)} %collective-permute-done.7.refs_8_) | copy-start | bytes 393220
  22.5 2.5 %collective-permute-start.4 = (bf16[256,256]{1,0:T(8,128)(2,1)S(1)}, bf16[256,256]{1,0:T(8,128)(2,1)S(1)}, u32[]{:S(2)}, u32[]{:S(2)}) collective-permute-start(bf16[256,256]{1,0:T(8,128)(2,1)S(1)} %collective-permute-done.3.refs_4_), channel_id=1, source_target_pairs={{0,1},{1,0},{2,3},{3,2},{4,5},{5,4},{6,7},{7,6},{8,9},{9,8},{10,11... | collective-permute-start | bytes 393224 | tf_op jit(solution)/shard_map/ppermute | solution.py:183
  22.5 10.1 %copy-start.5 = (bf16[256,256]{1,0:T(8,128)(2,1)}, bf16[256,256]{1,0:T(8,128)(2,1)S(1)}, u32[]{:S(2)}) copy-start(bf16[256,256]{1,0:T(8,128)(2,1)S(1)} %collective-permute-done.11.refs_12_) | copy-start | bytes 393220
  22.5 6.4 %collective-permute-start.9 = (bf16[256,256]{1,0:T(8,128)(2,1)S(1)}, bf16[256,256]{1,0:T(8,128)(2,1)S(1)}, u32[]{:S(2)}, u32[]{:S(2)}) collective-permute-start(bf16[256,256]{1,0:T(8,128)(2,1)S(1)} %collective-permute-done.7.refs_8_), channel_id=1, source_target_pairs={{0,2},{1,3},{2,0},{3,1},{4,6},{5,7},{6,4},{7,5},{8,10},{9,11},{10,... | collective-permute-start | bytes 393224 | tf_op jit(solution)/shard_map/ppermute | solution.py:183
  23.1 9.5 %copy-start.1 = (bf16[256,256]{1,0:T(8,128)(2,1)}, bf16[256,256]{1,0:T(8,128)(2,1)S(1)}, u32[]{:S(2)}) copy-start(bf16[256,256]{1,0:T(8,128)(2,1)S(1)} %collective-permute-done.1.refs_2_) | copy-start | bytes 393220
  23.1 5.9 %collective-permute-start.8 = (bf16[256,256]{1,0:T(8,128)(2,1)S(1)}, bf16[256,256]{1,0:T(8,128)(2,1)S(1)}, u32[]{:S(2)}, u32[]{:S(2)}) collective-permute-start(bf16[256,256]{1,0:T(8,128)(2,1)S(1)} %collective-permute-done.7.refs_8_), channel_id=1, source_target_pairs={{0,1},{1,0},{2,3},{3,2},{4,5},{5,4},{6,7},{7,6},{8,9},{9,8},{10,11... | collective-permute-start | bytes 393224 | tf_op jit(solution)/shard_map/ppermute | solution.py:183
  23.2 9.4 %copy-start.2 = (bf16[256,256]{1,0:T(8,128)(2,1)}, bf16[256,256]{1,0:T(8,128)(2,1)S(1)}, u32[]{:S(2)}) copy-start(bf16[256,256]{1,0:T(8,128)(2,1)S(1)} %collective-permute-done.refs_1_) | copy-start | bytes 393220
  23.3 8.0 %collective-permute-start.13 = (bf16[256,256]{1,0:T(8,128)(2,1)S(1)}, bf16[256,256]{1,0:T(8,128)(2,1)S(1)}, u32[]{:S(2)}, u32[]{:S(2)}) collective-permute-start(bf16[256,256]{1,0:T(8,128)(2,1)S(1)} %collective-permute-done.11.refs_12_), channel_id=1, source_target_pairs={{0,2},{1,3},{2,0},{3,1},{4,6},{5,7},{6,4},{7,5},{8,10},{9,11},{10,... | collective-permute-start | bytes 393224 | tf_op jit(solution)/shard_map/ppermute | solution.py:183
  24.9 7.8 %copy-start.6 = (bf16[256,256]{1,0:T(8,128)(2,1)}, bf16[256,256]{1,0:T(8,128)(2,1)S(1)}, u32[]{:S(2)}) copy-start(bf16[256,256]{1,0:T(8,128)(2,1)S(1)} %collective-permute-done.5.refs_6_) | copy-start | bytes 393220
  24.9 7.0 %collective-permute-start.12 = (bf16[256,256]{1,0:T(8,128)(2,1)S(1)}, bf16[256,256]{1,0:T(8,128)(2,1)S(1)}, u32[]{:S(2)}, u32[]{:S(2)}) collective-permute-start(bf16[256,256]{1,0:T(8,128)(2,1)S(1)} %collective-permute-done.11.refs_12_), channel_id=1, source_target_pairs={{0,1},{1,0},{2,3},{3,2},{4,5},{5,4},{6,7},{7,6},{8,9},{9,8},{10,11... | collective-permute-start | bytes 393224 | tf_op jit(solution)/shard_map/ppermute | solution.py:183
  25.0 7.6 %copy-start.7 = (bf16[256,256]{1,0:T(8,128)(2,1)}, bf16[256,256]{1,0:T(8,128)(2,1)S(1)}, u32[]{:S(2)}) copy-start(bf16[256,256]{1,0:T(8,128)(2,1)S(1)} %collective-permute-done.4.refs_5_) | copy-start | bytes 393220
  25.0 6.9 %collective-permute-start.2 = (bf16[256,256]{1,0:T(8,128)(2,1)S(1)}, bf16[256,256]{1,0:T(8,128)(2,1)S(1)}, u32[]{:S(2)}, u32[]{:S(2)}) collective-permute-start(bf16[256,256]{1,0:T(8,128)(2,1)S(1)} %collective-permute-done.1.refs_2_), channel_id=1, source_target_pairs={{0,1},{1,0},{2,3},{3,2},{4,5},{5,4},{6,7},{7,6},{8,9},{9,8},{10,11... | collective-permute-start | bytes 393224 | tf_op jit(solution)/shard_map/ppermute | solution.py:183
  29.0 3.7 %copy-start.8 = (bf16[256,256]{1,0:T(8,128)(2,1)}, bf16[256,256]{1,0:T(8,128)(2,1)S(1)}, u32[]{:S(2)}) copy-start(bf16[256,256]{1,0:T(8,128)(2,1)S(1)} %collective-permute-done.9.refs_10_) | copy-start | bytes 393220
  29.0 3.0 %collective-permute-start.6 = (bf16[256,256]{1,0:T(8,128)(2,1)S(1)}, bf16[256,256]{1,0:T(8,128)(2,1)S(1)}, u32[]{:S(2)}, u32[]{:S(2)}) collective-permute-start(bf16[256,256]{1,0:T(8,128)(2,1)S(1)} %collective-permute-done.5.refs_6_), channel_id=1, source_target_pairs={{0,1},{1,0},{2,3},{3,2},{4,5},{5,4},{6,7},{7,6},{8,9},{9,8},{10,11... | collective-permute-start | bytes 393224 | tf_op jit(solution)/shard_map/ppermute | solution.py:183
  29.0 3.7 %copy-start.9 = (bf16[256,256]{1,0:T(8,128)(2,1)}, bf16[256,256]{1,0:T(8,128)(2,1)S(1)}, u32[]{:S(2)}) copy-start(bf16[256,256]{1,0:T(8,128)(2,1)S(1)} %collective-permute-done.8.refs_9_) | copy-start | bytes 393220
  29.0 3.0 %collective-permute-start.10 = (bf16[256,256]{1,0:T(8,128)(2,1)S(1)}, bf16[256,256]{1,0:T(8,128)(2,1)S(1)}, u32[]{:S(2)}, u32[]{:S(2)}) collective-permute-start(bf16[256,256]{1,0:T(8,128)(2,1)S(1)} %collective-permute-done.9.refs_10_), channel_id=1, source_target_pairs={{0,1},{1,0},{2,3},{3,2},{4,5},{5,4},{6,7},{7,6},{8,9},{9,8},{10,11... | collective-permute-start | bytes 393224 | tf_op jit(solution)/shard_map/ppermute | solution.py:183
  31.2 1.4 %copy-start.10 = (bf16[256,256]{1,0:T(8,128)(2,1)}, bf16[256,256]{1,0:T(8,128)(2,1)S(1)}, u32[]{:S(2)}) copy-start(bf16[256,256]{1,0:T(8,128)(2,1)S(1)} %collective-permute-done.13.refs_14_) | copy-start | bytes 393220
  31.2 1.3 %collective-permute-start.14 = (bf16[256,256]{1,0:T(8,128)(2,1)S(1)}, bf16[256,256]{1,0:T(8,128)(2,1)S(1)}, u32[]{:S(2)}, u32[]{:S(2)}) collective-permute-start(bf16[256,256]{1,0:T(8,128)(2,1)S(1)} %collective-permute-done.13.refs_14_), channel_id=1, source_target_pairs={{0,1},{1,0},{2,3},{3,2},{4,5},{5,4},{6,7},{7,6},{8,9},{9,8},{10,11... | collective-permute-start | bytes 393224 | tf_op jit(solution)/shard_map/ppermute | solution.py:183
  31.9 0.8 %copy-start.11 = (bf16[256,256]{1,0:T(8,128)(2,1)}, bf16[256,256]{1,0:T(8,128)(2,1)S(1)}, u32[]{:S(2)}) copy-start(bf16[256,256]{1,0:T(8,128)(2,1)S(1)} %collective-permute-done.12.refs_13_) | copy-start | bytes 393220
  31.9 0.8 %copy-start.12 = (bf16[256,256]{1,0:T(8,128)(2,1)}, bf16[256,256]{1,0:T(8,128)(2,1)S(1)}, u32[]{:S(2)}) copy-start(bf16[256,256]{1,0:T(8,128)(2,1)S(1)} %collective-permute-done.2.refs_3_) | copy-start | bytes 393220
  31.9 0.8 %copy-start.13 = (bf16[256,256]{1,0:T(8,128)(2,1)}, bf16[256,256]{1,0:T(8,128)(2,1)S(1)}, u32[]{:S(2)}) copy-start(bf16[256,256]{1,0:T(8,128)(2,1)S(1)} %collective-permute-done.6.refs_7_) | copy-start | bytes 393220
  31.9 0.8 %copy-start.14 = (bf16[256,256]{1,0:T(8,128)(2,1)}, bf16[256,256]{1,0:T(8,128)(2,1)S(1)}, u32[]{:S(2)}) copy-start(bf16[256,256]{1,0:T(8,128)(2,1)S(1)} %collective-permute-done.10.refs_11_) | copy-start | bytes 393220
  32.7 0.7 copy-start.15
  50.1 8.3 %collective-permute-start.15 = (bf16[256,256]{1,0:T(8,128)(2,1)}, bf16[256,256]{1,0:T(8,128)(2,1)S(1)}, u32[]{:S(2)}, u32[]{:S(2)}) collective-permute-start(bf16[256,256]{1,0:T(8,128)(2,1)} %get-tuple-element.18), channel_id=1, source_target_pairs={{0,4},{1,5},{2,6},{3,7},{4,0},{5,1},{6,2},{7,3},{8,12},{9,13},{10,... | collective-permute-start | bytes 393224 | tf_op jit(solution)/shard_map/ppermute | solution.py:183
  51.8 13.1 %collective-permute-start.16 = (bf16[256,256]{1,0:T(8,128)(2,1)}, bf16[256,256]{1,0:T(8,128)(2,1)S(1)}, u32[]{:S(2)}, u32[]{:S(2)}) collective-permute-start(bf16[256,256]{1,0:T(8,128)(2,1)} %get-tuple-element.19), channel_id=1, source_target_pairs={{0,8},{1,9},{2,10},{3,11},{4,12},{5,13},{6,14},{7,15},{8,0},{9,1},... | collective-permute-start | bytes 393224 | tf_op jit(solution)/shard_map/ppermute | solution.py:183
  53.1 11.8 %collective-permute-start.17 = (bf16[256,256]{1,0:T(8,128)(2,1)}, bf16[256,256]{1,0:T(8,128)(2,1)S(1)}, u32[]{:S(2)}, u32[]{:S(2)}) collective-permute-start(bf16[256,256]{1,0:T(8,128)(2,1)} %get-tuple-element.20), channel_id=1, source_target_pairs={{0,12},{1,13},{2,14},{3,15},{4,8},{5,9},{6,10},{7,11},{8,4},{9,5},... | collective-permute-start | bytes 393224 | tf_op jit(solution)/shard_map/ppermute | solution.py:183
  58.4 6.6 %copy-start.16 = (bf16[256,256]{1,0:T(8,128)(2,1)}, bf16[256,256]{1,0:T(8,128)(2,1)S(1)}, u32[]{:S(2)}) copy-start(bf16[256,256]{1,0:T(8,128)(2,1)S(1)} %collective-permute-done.15.refs_1_) | copy-start | bytes 393220
  64.9 0.6 copy-start.17
  64.9 0.7 %copy-start.18 = (bf16[256,256]{1,0:T(8,128)(2,1)}, bf16[256,256]{1,0:T(8,128)(2,1)S(1)}, u32[]{:S(2)}) copy-start(bf16[256,256]{1,0:T(8,128)(2,1)S(1)} %collective-permute-done.17.refs_3_) | copy-start | bytes 393220
where the time goes:
time: 68.2 us; the launch traced here: 68 us
  waiting for transfers between devices  25 us (37%)
  Pallas kernels  22 us (32%)
  starting transfers between devices  15.5 us (23%)
  local copies, waits for them, and re-layouts  3.98 us (6%)
  other arithmetic  1.4 us (2%)
    ppermute x18, waiting for transfers between devices, swap(): return lax.ppermute(value, 'row', [(r, r ^ bits) for r in range(rows)])  25 us
    pallas_call x1, Pallas kernels, third(): pl.pallas_call(functools.partial(third_kernel, layout), in_specs=[vmem] *...  16.7 us
    ppermute x18, starting transfers between devices, swap(): return lax.ppermute(value, 'row', [(r, r ^ bits) for r in range(rows)])  15.5 us
    pallas_call x1, Pallas kernels, whiten(): pl.pallas_call(whiten_kernel, grid_spec=pltpu.PrefetchScalarGridSpec(num_...  2.87 us
    pallas_call x1, Pallas kernels, finish(): pl.pallas_call(finish_kernel, in_specs=[pl.BlockSpec(memory_space=pltpu.S...  2.35 us
    unnamed x42, local copies, waits for them, and re-layouts  2.14 us
  transfers between devices with their start and end apart: 18, of which 7 were waited for; matrix products, arithmetic and copies ran while one was open for 3% of the time, Pallas kernels for 0%

commit v1 on v0

v1 whole, which is shorter than its diff:
```python
import functools

import jax
import jax.numpy as jnp
from jax import lax
from jax.experimental import pallas as pl
from jax.experimental.pallas import tpu as pltpu
from jax.sharding import PartitionSpec as P

NTGT = 128
NT_DIMS = (((1,), (1,)), ((), ()))
F32, BF16 = jnp.float32, jnp.bfloat16
VMEM = pl.BlockSpec(memory_space=pltpu.VMEM)
SMEM = pl.BlockSpec(memory_space=pltpu.SMEM)
ANY = pl.BlockSpec(memory_space=pl.ANY)


def whiten_kernel(spread, bins, spectra, *refs):
    count = len(refs) - 2
    outs, held, sems = refs[:count], refs[count], refs[count + 1]
    mine = lax.axis_index("row") // spread
    copies = [
        pltpu.make_async_copy(spectra.at[:, bins[mine ^ slot]], held.at[slot], sems.at[slot])
        for slot in range(count)
    ]
    for copy in copies:
        copy.start()
    for slot in range(count):
        copies[slot].wait()
        real, imag = held[slot, 0], held[slot, 1]
        power = jnp.mean(real * real + imag * imag, axis=1, keepdims=True)
        scale = 1.0 / jnp.sqrt(power + 1e-06)
        outs[slot][...] = jnp.concatenate([real * scale, imag * scale], axis=1).astype(BF16)


def whiten(spectra, bins, spread):
    _, _, own, windows = spectra.shape
    count = bins.shape[0]
    return pl.pallas_call(
        functools.partial(whiten_kernel, spread),
        in_specs=[SMEM, ANY],
        out_specs=[VMEM] * count,
        out_shape=[jax.ShapeDtypeStruct((own, 2 * windows), BF16)] * count,
        scratch_shapes=[
            pltpu.VMEM((count, 2, own, windows), F32),
            pltpu.SemaphoreType.DMA((count,)),
        ],
        name="whiten",
    )(bins, spectra)


def quarter_turn(rows):
    half = rows.shape[1] // 2
    return jnp.concatenate([rows[:, half:], -rows[:, :half]], axis=1)


def source_row(spread, slot, held):
    me = lax.axis_index("row")
    return ((me // spread) ^ slot) * spread + ((me % spread) ^ held)


def plan_kernel(layout, mask_s, mask_v, after, weights, subset):
    count, spread, own, spacing, grp = layout
    per = own // grp
    groups = mask_v.shape[0]
    table = mask_v[...].astype(F32).astype(BF16)
    rowg = (lax.broadcasted_iota(jnp.int32, (2 * NTGT, groups), 0) % NTGT) * spacing // grp
    rowpick = (rowg == lax.broadcasted_iota(jnp.int32, rowg.shape, 1)).astype(F32).astype(BF16)
    by_target = jnp.dot(rowpick, table, preferred_element_type=F32).astype(BF16)

    def block_body(at, carry):
        first_group = source_row(spread, at // spread, at % spread) * per
        lanes = first_group + lax.broadcasted_iota(jnp.int32, (groups, own), 1) // grp
        onehot = (lanes == lax.broadcasted_iota(jnp.int32, (groups, own), 0)).astype(F32).astype(BF16)
        weights[at] = jnp.dot(by_target, onehot, preferred_element_type=F32).astype(BF16)
        for slot in range(count):
            for part in range(per):
                group = source_row(spread, slot, 0) * per + part
                bits = mask_s[group, first_group]
                for b in range(1, per):
                    bits = bits + mask_s[group, first_group + b] * (1 << b)
                subset[at, slot * per + part] = bits
        return carry

    lax.fori_loop(0, count * spread, block_body, 0)


def plan(mask, after, layout):
    count, spread, own, spacing, grp = layout
    return pl.pallas_call(
        functools.partial(plan_kernel, layout),
        in_specs=[SMEM, VMEM, ANY],
        out_specs=[VMEM, SMEM],
        out_shape=[
            jax.ShapeDtypeStruct((count * spread, 2 * NTGT, own), BF16),
            jax.ShapeDtypeStruct((count * spread, count * own // grp), jnp.int32),
        ],
        name="plan",
    )(mask, mask, after)


def third_kernel(layout, subset, weights, *refs):
    count, spread, own, spacing, grp = layout
    blocks = refs[: count * spread]
    outs = refs[count * spread : count * spread + count]
    everyone, trows, both, tables, moved = refs[count * spread + count :]
    per, width, tper = own // grp, everyone.shape[-1], own // spacing
    half = width // 2
    for held in range(spread):
        for slot in range(count):
            block = blocks[slot * spread + held]
            everyone[held * count + slot] = block[...]
            row = source_row(spread, slot, held)
            for j in range(tper):
                trows[pl.ds(row * tper + j, 1), :] = block[pl.ds(j * spacing, 1), :].astype(F32)
    targets = trows[...].astype(BF16)
    both[0:NTGT] = targets
    both[NTGT:] = quarter_turn(targets)
    moved[...] = jnp.zeros_like(moved)
    for slot in range(count):
        tables[slot, 0] = jnp.zeros(tables.shape[2:], F32)
    lane = lax.broadcasted_iota(jnp.int32, (1, own), 1) // grp
    only = [jnp.where(lane == part, 1.0, 0.0).astype(BF16) for part in range(per)]

    def held_body(held, carry):
        for slot in range(count):
            block = everyone[held * count + slot]
            at = slot * spread + held
            corr = lax.dot_general(both[...], block, NT_DIMS, preferred_element_type=F32)
            corr = corr.astype(BF16) * weights[at]
            for part in range(per):
                v = jnp.dot(corr * only[part], block, preferred_element_type=F32)
                real = v[:NTGT, :half] - v[NTGT:, half:]
                imag = -(v[NTGT:, :half] + v[:NTGT, half:])
                one = jnp.concatenate([real, imag], axis=1)
                tables[slot, 1 << part] = one
                for low in range(1, 1 << part):
                    tables[slot, (1 << part) + low] = tables[slot, low] + one
        for group in range(count * per):
            total = tables[0, subset[held, group]]
            for slot in range(1, count):
                total = total + tables[slot, subset[slot * spread + held, group]]
            moved[group] += total
        return carry

    lax.fori_loop(0, spread, held_body, 0)
    for slot in range(count):
        left = blocks[slot * spread][...]
        for part in range(per):
            u = moved[slot * per + part]
            real, imag = u[:, :half], u[:, half:]
            right = jnp.concatenate(
                [jnp.concatenate([real, -imag], axis=1), jnp.concatenate([imag, real], axis=1)], axis=0
            ).astype(BF16)
            result = lax.dot_general(
                left[part * grp : (part + 1) * grp], right, NT_DIMS, preferred_element_type=F32
            )
            outs[slot][pl.ds(part * grp, grp), :] = (result * (1.0 / (half * half))).astype(BF16)


def third(blocks, subset, weights, layout):
    count, spread, own, spacing, grp = layout
    width = blocks[0].shape[-1]
    per = own // grp
    return pl.pallas_call(
        functools.partial(third_kernel, layout),
        in_specs=[SMEM, VMEM] + [VMEM] * (count * spread),
        out_specs=[VMEM] * count,
        out_shape=[jax.ShapeDtypeStruct((own, 2 * NTGT), BF16)] * count,
        scratch_shapes=[
            pltpu.VMEM((spread * count, own, width), BF16),
            pltpu.VMEM((NTGT, width), F32),
            pltpu.VMEM((2 * NTGT, width), BF16),
            pltpu.VMEM((count, 1 << per, NTGT, width), F32),
            pltpu.VMEM((count * per, NTGT, width), F32),
        ],
        name="third",
    )(subset, weights, *blocks)


def finish_kernel(spread, *refs):
    blocks, out = refs[:-1], refs[-1]
    count = len(blocks)
    own = blocks[0].shape[0]
    mine = lax.axis_index("row") // spread
    for slot, block in enumerate(blocks):
        value = block[...].astype(F32)
        for part in range(2):
            out[pl.ds(part * count + (mine ^ slot), own, stride=2 * count), :] = value[
                :, part * NTGT : (part + 1) * NTGT
            ]


def finish(blocks, spread):
    own = blocks[0].shape[0]
    count = len(blocks)
    out = pl.pallas_call(
        functools.partial(finish_kernel, spread),
        in_specs=[VMEM] * count,
        out_specs=VMEM,
        out_shape=jax.ShapeDtypeStruct((own * 2 * count, NTGT), F32),
        name="finish",
    )(*blocks)
    return out.reshape(own, 2, count, NTGT)


def on_device(rows, spectra, coda_bins, source_mask):
    count = coda_bins.shape[0]
    spread = rows // count
    own = spectra.shape[2]
    channels = own * rows
    layout = (count, spread, own, channels // NTGT, channels // source_mask.shape[0])

    def swap(value, bits):
        return lax.ppermute(value, "row", [(r, r ^ bits) for r in range(rows)])

    white = whiten(spectra, coda_bins, spread)
    weights, subset = plan(source_mask, white[0], layout)
    blocks = [[white[0]] + [None] * (spread - 1)]
    for slot in range(1, count):
        blocks.append([swap(white[slot], slot * spread)] + [None] * (spread - 1))
    bit = spread // 2
    while bit >= 1:
        for slot in range(count):
            for held in range(0, spread, 2 * bit):
                blocks[slot][held + bit] = swap(blocks[slot][held], bit)
        bit //= 2
    flat = [blocks[slot][held] for slot in range(count) for held in range(spread)]
    parts = third(flat, subset, weights, layout)
    back = [parts[0]] + [swap(parts[slot], slot * spread) for slot in range(1, count)]
    return finish(back, spread)


def solution(mesh):
    return jax.shard_map(
        functools.partial(on_device, mesh.shape["row"]),
        mesh=mesh,
        in_specs=(P(None, None, "row", "band"), P("band"), P("band", None)),
        out_specs=P(("band", "row"), None, None, None),
        check_vma=False,
    )
```

time: 68.2 us -> 63.9 us (0.937)
  waiting for transfers between devices: 25 us -> 22.3 us
  local copies, waits for them, and re-layouts: 3.98 us -> 1.41 us
  other arithmetic: 1.4 us -> 0 us
  starting transfers between devices: 15.5 us -> 16.8 us
  Pallas kernels: 22 us -> 22.8 us
    ppermute x18, waiting for transfers between devices: 25 us -> 22.3 us  [swap(): return lax.ppermute(value, 'row', [(r, r ^ bits) for r in range(rows)])]
    ppermute x18, starting transfers between devices: 15.5 us -> 16.8 us  [swap(): return lax.ppermute(value, 'row', [(r, r ^ bits) for r in range(rows)])]
    gather x1 -> x0, local copies, waits for them, and re-layouts: 1.17 us -> none  [on_device(): white = whiten(spectra, coda_bins[place])]
    pallas_call x3 -> x4, Pallas kernels: 22 us -> 22.8 us  [the longest x1 12 us: third(): pl.pallas_call(functools.partial(third_kernel, layout), in_specs=[SMEM, V...]
    unnamed x42 -> x36, local copies, waits for them, and re-layouts: 2.14 us -> 1.41 us
    add x2 -> x0, other arithmetic: 0.73 us -> none  [the longest x1 0.66 us: on_device(): source[:, :, None] * own + jnp.arange(own, dtype=jnp.int32)]
  transfers between devices with their start and end apart: 18 -> 18, of which waited for: 7 -> 6; matrix products, arithmetic and copies ran while one was open for 3% -> 0% of each run, Pallas kernels for 0% -> 9%
where the time goes in v1:
time: 63.9 us; the launch traced here: 63.6 us
  Pallas kernels  22.8 us (36%)
  waiting for transfers between devices  22.3 us (35%)
  starting transfers between devices  16.8 us (26%)
  local copies, waits for them, and re-layouts  1.41 us (2%)
    ppermute x18, waiting for transfers between devices, swap(): return lax.ppermute(value, 'row', [(r, r ^ bits) for r in range(rows)])  22.3 us
    ppermute x18, starting transfers between devices, swap(): return lax.ppermute(value, 'row', [(r, r ^ bits) for r in range(rows)])  16.8 us
    pallas_call x1, Pallas kernels, third(): pl.pallas_call(functools.partial(third_kernel, layout), in_specs=[SMEM, V...  12 us
    pallas_call x1, Pallas kernels, plan(): pl.pallas_call(functools.partial(plan_kernel, layout), in_specs=[SMEM, VM...  5.62 us
    pallas_call x1, Pallas kernels, whiten(): pl.pallas_call(functools.partial(whiten_kernel, spread), in_specs=[SMEM,...  2.9 us
    pallas_call x1, Pallas kernels, finish(): pl.pallas_call(functools.partial(finish_kernel, spread), in_specs=[VMEM]...  2.34 us
    unnamed x36, local copies, waits for them, and re-layouts  1.41 us
  transfers between devices with their start and end apart: 18, of which 6 were waited for; matrix products, arithmetic and copies ran while one was open for 0% of the time, Pallas kernels for 9%

profile of v1, /device:TPU:0, one launch (start us, length us, event | category | flops | bytes accessed | tf_op | source)
XLA Modules:
  0.0 63.6 jit_solution(13231856698281826203)
XLA Ops:
  0.0 2.9 %whiten.1 = (bf16[256,256]{1,0:T(8,128)(2,1)}, bf16[256,256]{1,0:T(8,128)(2,1)}, bf16[256,256]{1,0:T(8,128)(2,1)}, bf16[256,256]{1,0:T(8,128)(2,1)}) custom-call(s32[4]{0:T(128)} %bins.1, f32[2,16,256,128]{3,2,1,0:T(8,128)} %spectra.1), custom_call_target="tpu_custom_call" | custom-call | tf_op jit(solution)/shard_map/whiten/pallas_call | solution.py:39
  2.9 3.1 %collective-permute-start.3 = (bf16[256,256]{1,0:T(8,128)(2,1)}, bf16[256,256]{1,0:T(8,128)(2,1)S(1)}, u32[]{:S(2)}, u32[]{:S(2)}) collective-permute-start(bf16[256,256]{1,0:T(8,128)(2,1)} %get-tuple-element.18), channel_id=1, source_target_pairs={{0,4},{1,5},{2,6},{3,7},{4,0},{5,1},{6,2},{7,3},{8,12},{9,13},{10,... | collective-permute-start | bytes 393224 | tf_op jit(solution)/shard_map/ppermute | solution.py:215
  6.0 2.6 %collective-permute-start.7 = (bf16[256,256]{1,0:T(8,128)(2,1)}, bf16[256,256]{1,0:T(8,128)(2,1)S(1)}, u32[]{:S(2)}, u32[]{:S(2)}) collective-permute-start(bf16[256,256]{1,0:T(8,128)(2,1)} %get-tuple-element.19), channel_id=1, source_target_pairs={{0,8},{1,9},{2,10},{3,11},{4,12},{5,13},{6,14},{7,15},{8,0},{9,1},... | collective-permute-start | bytes 393224 | tf_op jit(solution)/shard_map/ppermute | solution.py:215
  8.6 0.0 collective-permute-start.11
  8.6 1.7 %collective-permute-start.1 = (bf16[256,256]{1,0:T(8,128)(2,1)}, bf16[256,256]{1,0:T(8,128)(2,1)S(1)}, u32[]{:S(2)}, u32[]{:S(2)}) collective-permute-start(bf16[256,256]{1,0:T(8,128)(2,1)} %get-tuple-element.15.after.refs_0_), channel_id=1, source_target_pairs={{0,2},{1,3},{2,0},{3,1},{4,6},{5,7},{6,4},{7,5},{8,10},{9,11},{10,... | collective-permute-start | bytes 393224 | tf_op jit(solution)/shard_map/ppermute | solution.py:215
  10.4 0.0 collective-permute-start
  10.4 1.0 %collective-permute-done.3.refs_4_ = bf16[256,256]{1,0:T(8,128)(2,1)S(1)} collective-permute-done((bf16[256,256]{1,0:T(8,128)(2,1)}, bf16[256,256]{1,0:T(8,128)(2,1)S(1)}, u32[]{:S(2)}, u32[]{:S(2)}) %collective-permute-start.3) | collective-permute-done | bytes 131104 | tf_op jit(solution)/shard_map/ppermute | solution.py:215
  11.3 1.7 %collective-permute-start.5 = (bf16[256,256]{1,0:T(8,128)(2,1)S(1)}, bf16[256,256]{1,0:T(8,128)(2,1)S(1)}, u32[]{:S(2)}, u32[]{:S(2)}) collective-permute-start(bf16[256,256]{1,0:T(8,128)(2,1)S(1)} %collective-permute-done.3.refs_4_), channel_id=1, source_target_pairs={{0,2},{1,3},{2,0},{3,1},{4,6},{5,7},{6,4},{7,5},{8,10},{9,11},{10,... | collective-permute-start | bytes 393224 | tf_op jit(solution)/shard_map/ppermute | solution.py:215
  13.1 6.1 %collective-permute-done.7.refs_8_ = bf16[256,256]{1,0:T(8,128)(2,1)S(1)} collective-permute-done((bf16[256,256]{1,0:T(8,128)(2,1)}, bf16[256,256]{1,0:T(8,128)(2,1)S(1)}, u32[]{:S(2)}, u32[]{:S(2)}) %collective-permute-start.7) | collective-permute-done | bytes 131104 | tf_op jit(solution)/shard_map/ppermute | solution.py:215
  19.1 0.0 collective-permute-start.4
  19.1 0.0 collective-permute-done.11.refs_12_
  19.1 1.6 %collective-permute-start.9 = (bf16[256,256]{1,0:T(8,128)(2,1)S(1)}, bf16[256,256]{1,0:T(8,128)(2,1)S(1)}, u32[]{:S(2)}, u32[]{:S(2)}) collective-permute-start(bf16[256,256]{1,0:T(8,128)(2,1)S(1)} %collective-permute-done.7.refs_8_), channel_id=1, source_target_pairs={{0,2},{1,3},{2,0},{3,1},{4,6},{5,7},{6,4},{7,5},{8,10},{9,11},{10,... | collective-permute-start | bytes 393224 | tf_op jit(solution)/shard_map/ppermute | solution.py:215
  20.7 0.0 collective-permute-done.1.refs_2_
  20.7 0.2 collective-permute-start.8
  20.9 0.0 collective-permute-done.refs_1_
  20.9 0.5 collective-permute-start.13
  21.4 0.0 collective-permute-done.5.refs_6_
  21.4 0.1 collective-permute-start.12
  21.5 0.0 collective-permute-done.4.refs_5_
  21.5 0.4 collective-permute-start.2
  21.9 3.7 %collective-permute-done.9.refs_10_ = bf16[256,256]{1,0:T(8,128)(2,1)S(1)} collective-permute-done((bf16[256,256]{1,0:T(8,128)(2,1)S(1)}, bf16[256,256]{1,0:T(8,128)(2,1)S(1)}, u32[]{:S(2)}, u32[]{:S(2)}) %collective-permute-start.9) | collective-permute-done | bytes 131104 | tf_op jit(solution)/shard_map/ppermute | solution.py:215
  25.6 0.0 collective-permute-start.6
  25.6 0.0 collective-permute-done.8.refs_9_
  25.6 0.5 collective-permute-start.10
  26.1 1.8 %collective-permute-done.13.refs_14_ = bf16[256,256]{1,0:T(8,128)(2,1)S(1)} collective-permute-done((bf16[256,256]{1,0:T(8,128)(2,1)S(1)}, bf16[256,256]{1,0:T(8,128)(2,1)S(1)}, u32[]{:S(2)}, u32[]{:S(2)}) %collective-permute-start.13) | collective-permute-done | bytes 131104 | tf_op jit(solution)/shard_map/ppermute | solution.py:215
  27.9 0.0 collective-permute-start.14
  27.9 5.6 %plan.1 = (bf16[16,256,256]{2,1,0:T(8,128)(2,1)}, s32[16,16]{1,0:T(8,128)}) custom-call(s32[64,64]{1,0:T(8,128)} %mask_v.1, s32[64,64]{1,0:T(8,128)} %mask_v.1, bf16[256,256]{1,0:T(8,128)(2,1)} %get-tuple-element.15.after.refs_0_), custom_call_target="tpu_custom_call" | custom-call | tf_op jit(solution)/shard_map/plan/pallas_call | solution.py:90
  33.5 0.0 collective-permute-done.12.refs_13_
  33.5 0.0 collective-permute-done.2.refs_3_
  33.5 0.0 collective-permute-done.6.refs_7_
  33.5 0.0 copy-start.12
  33.5 0.0 collective-permute-done.10.refs_11_
  33.6 0.0 collective-permute-done.14.refs_15_
  33.7 0.5 copy-done.10
  34.2 0.0 copy-done.11
  34.2 0.1 copy-done.12
  34.3 0.0 copy-done.13
  34.3 0.1 copy-done.14
  34.4 12.0 %third.1 = (bf16[256,256]{1,0:T(8,128)(2,1)}, bf16[256,256]{1,0:T(8,128)(2,1)}, bf16[256,256]{1,0:T(8,128)(2,1)}, bf16[256,256]{1,0:T(8,128)(2,1)}) custom-call(s32[16,16]{1,0:T(8,128)} %get-tuple-element.16.subset, bf16[16,256,256]{2,1,0:T(8,128)(2,1)} %get-tuple-element.17.weights, bf16[256,256]{1,0:T(8,128)(2,1)} %get-tuple-element.15.after.refs_0_, ...), custom_call_target="tpu_custom_call" | custom-call | tf_op jit(solution)/shard_map/third/pallas_call | solution.py:165
  46.3 1.1 %collective-permute-start.15 = (bf16[256,256]{1,0:T(8,128)(2,1)}, bf16[256,256]{1,0:T(8,128)(2,1)S(1)}, u32[]{:S(2)}, u32[]{:S(2)}) collective-permute-start(bf16[256,256]{1,0:T(8,128)(2,1)} %get-tuple-element.22), channel_id=1, source_target_pairs={{0,4},{1,5},{2,6},{3,7},{4,0},{5,1},{6,2},{7,3},{8,12},{9,13},{10,... | collective-permute-start | bytes 393224 | tf_op jit(solution)/shard_map/ppermute | solution.py:215
  47.4 1.8 %collective-permute-start.16 = (bf16[256,256]{1,0:T(8,128)(2,1)}, bf16[256,256]{1,0:T(8,128)(2,1)S(1)}, u32[]{:S(2)}, u32[]{:S(2)}) collective-permute-start(bf16[256,256]{1,0:T(8,128)(2,1)} %get-tuple-element.23), channel_id=1, source_target_pairs={{0,8},{1,9},{2,10},{3,11},{4,12},{5,13},{6,14},{7,15},{8,0},{9,1},... | collective-permute-start | bytes 393224 | tf_op jit(solution)/shard_map/ppermute | solution.py:215
  49.2 1.6 %collective-permute-start.17 = (bf16[256,256]{1,0:T(8,128)(2,1)}, bf16[256,256]{1,0:T(8,128)(2,1)S(1)}, u32[]{:S(2)}, u32[]{:S(2)}) collective-permute-start(bf16[256,256]{1,0:T(8,128)(2,1)} %get-tuple-element.24), channel_id=1, source_target_pairs={{0,12},{1,13},{2,14},{3,15},{4,8},{5,9},{6,10},{7,11},{8,4},{9,5},... | collective-permute-start | bytes 393224 | tf_op jit(solution)/shard_map/ppermute | solution.py:215
  50.7 4.1 %collective-permute-done.15.refs_1_ = bf16[256,256]{1,0:T(8,128)(2,1)S(1)} collective-permute-done((bf16[256,256]{1,0:T(8,128)(2,1)}, bf16[256,256]{1,0:T(8,128)(2,1)S(1)}, u32[]{:S(2)}, u32[]{:S(2)}) %collective-permute-start.15) | collective-permute-done | bytes 131104 | tf_op jit(solution)/shard_map/ppermute | solution.py:215
  54.8 5.7 %collective-permute-done.16.refs_2_ = bf16[256,256]{1,0:T(8,128)(2,1)S(1)} collective-permute-done((bf16[256,256]{1,0:T(8,128)(2,1)}, bf16[256,256]{1,0:T(8,128)(2,1)S(1)}, u32[]{:S(2)}, u32[]{:S(2)}) %collective-permute-start.16) | collective-permute-done | bytes 131104 | tf_op jit(solution)/shard_map/ppermute | solution.py:215
  60.5 0.0 collective-permute-done.17.refs_3_
  60.5 0.6 copy-done.16
  61.2 0.1 copy-done.17
  61.2 2.3 %finish.1 = f32[2048,128]{1,0:T(8,128)} custom-call(bf16[256,256]{1,0:T(8,128)(2,1)} %get-tuple-element.21.refs_0_, bf16[256,256]{1,0:T(8,128)(2,1)} %copy-done.15, bf16[256,256]{1,0:T(8,128)(2,1)} %copy-done.16, bf16[256,256]{1,0:T(8,128)(2,1)} %copy-done.17), custom_call_target="tpu_custom_call" | custom-call | tf_op jit(solution)/shard_map/finish/pallas_call | solution.py:197
  (28 shorter events, 0.1 us)
Async XLA Ops:
  2.9 8.4 %collective-permute-start.3 = (bf16[256,256]{1,0:T(8,128)(2,1)}, bf16[256,256]{1,0:T(8,128)(2,1)S(1)}, u32[]{:S(2)}, u32[]{:S(2)}) collective-permute-start(bf16[256,256]{1,0:T(8,128)(2,1)} %get-tuple-element.18), channel_id=1, source_target_pairs={{0,4},{1,5},{2,6},{3,7},{4,0},{5,1},{6,2},{7,3},{8,12},{9,13},{10,... | collective-permute-start | bytes 393224 | tf_op jit(solution)/shard_map/ppermute | solution.py:215
  6.0 13.1 %collective-permute-start.7 = (bf16[256,256]{1,0:T(8,128)(2,1)}, bf16[256,256]{1,0:T(8,128)(2,1)S(1)}, u32[]{:S(2)}, u32[]{:S(2)}) collective-permute-start(bf16[256,256]{1,0:T(8,128)(2,1)} %get-tuple-element.19), channel_id=1, source_target_pairs={{0,8},{1,9},{2,10},{3,11},{4,12},{5,13},{6,14},{7,15},{8,0},{9,1},... | collective-permute-start | bytes 393224 | tf_op jit(solution)/shard_map/ppermute | solution.py:215
  8.6 10.5 %collective-permute-start.11 = (bf16[256,256]{1,0:T(8,128)(2,1)}, bf16[256,256]{1,0:T(8,128)(2,1)S(1)}, u32[]{:S(2)}, u32[]{:S(2)}) collective-permute-start(bf16[256,256]{1,0:T(8,128)(2,1)} %get-tuple-element.20), channel_id=1, source_target_pairs={{0,12},{1,13},{2,14},{3,15},{4,8},{5,9},{6,10},{7,11},{8,4},{9,5},... | collective-permute-start | bytes 393224 | tf_op jit(solution)/shard_map/ppermute | solution.py:215
  8.6 12.1 %collective-permute-start.1 = (bf16[256,256]{1,0:T(8,128)(2,1)}, bf16[256,256]{1,0:T(8,128)(2,1)S(1)}, u32[]{:S(2)}, u32[]{:S(2)}) collective-permute-start(bf16[256,256]{1,0:T(8,128)(2,1)} %get-tuple-element.15.after.refs_0_), channel_id=1, source_target_pairs={{0,2},{1,3},{2,0},{3,1},{4,6},{5,7},{6,4},{7,5},{8,10},{9,11},{10,... | collective-permute-start | bytes 393224 | tf_op jit(solution)/shard_map/ppermute | solution.py:215
  10.4 10.5 %collective-permute-start = (bf16[256,256]{1,0:T(8,128)(2,1)}, bf16[256,256]{1,0:T(8,128)(2,1)S(1)}, u32[]{:S(2)}, u32[]{:S(2)}) collective-permute-start(bf16[256,256]{1,0:T(8,128)(2,1)} %get-tuple-element.15.after.refs_0_), channel_id=1, source_target_pairs={{0,1},{1,0},{2,3},{3,2},{4,5},{5,4},{6,7},{7,6},{8,9},{9,8},{10,11... | collective-permute-start | bytes 393224 | tf_op jit(solution)/shard_map/ppermute | solution.py:215
  11.3 22.3 %copy-start = (bf16[256,256]{1,0:T(8,128)(2,1)}, bf16[256,256]{1,0:T(8,128)(2,1)S(1)}, u32[]{:S(2)}) copy-start(bf16[256,256]{1,0:T(8,128)(2,1)S(1)} %collective-permute-done.3.refs_4_) | copy-start | bytes 393220
  11.3 10.1 %collective-permute-start.5 = (bf16[256,256]{1,0:T(8,128)(2,1)S(1)}, bf16[256,256]{1,0:T(8,128)(2,1)S(1)}, u32[]{:S(2)}, u32[]{:S(2)}) collective-permute-start(bf16[256,256]{1,0:T(8,128)(2,1)S(1)} %collective-permute-done.3.refs_4_), channel_id=1, source_target_pairs={{0,2},{1,3},{2,0},{3,1},{4,6},{5,7},{6,4},{7,5},{8,10},{9,11},{10,... | collective-permute-start | bytes 393224 | tf_op jit(solution)/shard_map/ppermute | solution.py:215
  19.1 14.5 %copy-start.1 = (bf16[256,256]{1,0:T(8,128)(2,1)}, bf16[256,256]{1,0:T(8,128)(2,1)S(1)}, u32[]{:S(2)}) copy-start(bf16[256,256]{1,0:T(8,128)(2,1)S(1)} %collective-permute-done.7.refs_8_) | copy-start | bytes 393220
  19.1 2.4 %collective-permute-start.4 = (bf16[256,256]{1,0:T(8,128)(2,1)S(1)}, bf16[256,256]{1,0:T(8,128)(2,1)S(1)}, u32[]{:S(2)}, u32[]{:S(2)}) collective-permute-start(bf16[256,256]{1,0:T(8,128)(2,1)S(1)} %collective-permute-done.3.refs_4_), channel_id=1, source_target_pairs={{0,1},{1,0},{2,3},{3,2},{4,5},{5,4},{6,7},{7,6},{8,9},{9,8},{10,11... | collective-permute-start | bytes 393224 | tf_op jit(solution)/shard_map/ppermute | solution.py:215
  19.1 14.5 %copy-start.2 = (bf16[256,256]{1,0:T(8,128)(2,1)}, bf16[256,256]{1,0:T(8,128)(2,1)S(1)}, u32[]{:S(2)}) copy-start(bf16[256,256]{1,0:T(8,128)(2,1)S(1)} %collective-permute-done.11.refs_12_) | copy-start | bytes 393220
  19.1 6.4 %collective-permute-start.9 = (bf16[256,256]{1,0:T(8,128)(2,1)S(1)}, bf16[256,256]{1,0:T(8,128)(2,1)S(1)}, u32[]{:S(2)}, u32[]{:S(2)}) collective-permute-start(bf16[256,256]{1,0:T(8,128)(2,1)S(1)} %collective-permute-done.7.refs_8_), channel_id=1, source_target_pairs={{0,2},{1,3},{2,0},{3,1},{4,6},{5,7},{6,4},{7,5},{8,10},{9,11},{10,... | collective-permute-start | bytes 393224 | tf_op jit(solution)/shard_map/ppermute | solution.py:215
  20.7 12.9 %copy-start.3 = (bf16[256,256]{1,0:T(8,128)(2,1)}, bf16[256,256]{1,0:T(8,128)(2,1)S(1)}, u32[]{:S(2)}) copy-start(bf16[256,256]{1,0:T(8,128)(2,1)S(1)} %collective-permute-done.1.refs_2_) | copy-start | bytes 393220
  20.7 4.9 %collective-permute-start.8 = (bf16[256,256]{1,0:T(8,128)(2,1)S(1)}, bf16[256,256]{1,0:T(8,128)(2,1)S(1)}, u32[]{:S(2)}, u32[]{:S(2)}) collective-permute-start(bf16[256,256]{1,0:T(8,128)(2,1)S(1)} %collective-permute-done.7.refs_8_), channel_id=1, source_target_pairs={{0,1},{1,0},{2,3},{3,2},{4,5},{5,4},{6,7},{7,6},{8,9},{9,8},{10,11... | collective-permute-start | bytes 393224 | tf_op jit(solution)/shard_map/ppermute | solution.py:215
  20.9 12.7 %copy-start.4 = (bf16[256,256]{1,0:T(8,128)(2,1)}, bf16[256,256]{1,0:T(8,128)(2,1)S(1)}, u32[]{:S(2)}) copy-start(bf16[256,256]{1,0:T(8,128)(2,1)S(1)} %collective-permute-done.refs_1_) | copy-start | bytes 393220
  20.9 7.0 %collective-permute-start.13 = (bf16[256,256]{1,0:T(8,128)(2,1)S(1)}, bf16[256,256]{1,0:T(8,128)(2,1)S(1)}, u32[]{:S(2)}, u32[]{:S(2)}) collective-permute-start(bf16[256,256]{1,0:T(8,128)(2,1)S(1)} %collective-permute-done.11.refs_12_), channel_id=1, source_target_pairs={{0,2},{1,3},{2,0},{3,1},{4,6},{5,7},{6,4},{7,5},{8,10},{9,11},{10,... | collective-permute-start | bytes 393224 | tf_op jit(solution)/shard_map/ppermute | solution.py:215
  21.4 12.2 %copy-start.5 = (bf16[256,256]{1,0:T(8,128)(2,1)}, bf16[256,256]{1,0:T(8,128)(2,1)S(1)}, u32[]{:S(2)}) copy-start(bf16[256,256]{1,0:T(8,128)(2,1)S(1)} %collective-permute-done.5.refs_6_) | copy-start | bytes 393220
  21.4 12.1 %collective-permute-start.12 = (bf16[256,256]{1,0:T(8,128)(2,1)S(1)}, bf16[256,256]{1,0:T(8,128)(2,1)S(1)}, u32[]{:S(2)}, u32[]{:S(2)}) collective-permute-start(bf16[256,256]{1,0:T(8,128)(2,1)S(1)} %collective-permute-done.11.refs_12_), channel_id=1, source_target_pairs={{0,1},{1,0},{2,3},{3,2},{4,5},{5,4},{6,7},{7,6},{8,9},{9,8},{10,11... | collective-permute-start | bytes 393224 | tf_op jit(solution)/shard_map/ppermute | solution.py:215
  21.5 12.2 %copy-start.6 = (bf16[256,256]{1,0:T(8,128)(2,1)}, bf16[256,256]{1,0:T(8,128)(2,1)S(1)}, u32[]{:S(2)}) copy-start(bf16[256,256]{1,0:T(8,128)(2,1)S(1)} %collective-permute-done.4.refs_5_) | copy-start | bytes 393220
  21.5 12.0 %collective-permute-start.2 = (bf16[256,256]{1,0:T(8,128)(2,1)S(1)}, bf16[256,256]{1,0:T(8,128)(2,1)S(1)}, u32[]{:S(2)}, u32[]{:S(2)}) collective-permute-start(bf16[256,256]{1,0:T(8,128)(2,1)S(1)} %collective-permute-done.1.refs_2_), channel_id=1, source_target_pairs={{0,1},{1,0},{2,3},{3,2},{4,5},{5,4},{6,7},{7,6},{8,9},{9,8},{10,11... | collective-permute-start | bytes 393224 | tf_op jit(solution)/shard_map/ppermute | solution.py:215
  25.6 8.1 %copy-start.7 = (bf16[256,256]{1,0:T(8,128)(2,1)}, bf16[256,256]{1,0:T(8,128)(2,1)S(1)}, u32[]{:S(2)}) copy-start(bf16[256,256]{1,0:T(8,128)(2,1)S(1)} %collective-permute-done.9.refs_10_) | copy-start | bytes 393220
  25.6 7.9 %collective-permute-start.6 = (bf16[256,256]{1,0:T(8,128)(2,1)S(1)}, bf16[256,256]{1,0:T(8,128)(2,1)S(1)}, u32[]{:S(2)}, u32[]{:S(2)}) collective-permute-start(bf16[256,256]{1,0:T(8,128)(2,1)S(1)} %collective-permute-done.5.refs_6_), channel_id=1, source_target_pairs={{0,1},{1,0},{2,3},{3,2},{4,5},{5,4},{6,7},{7,6},{8,9},{9,8},{10,11... | collective-permute-start | bytes 393224 | tf_op jit(solution)/shard_map/ppermute | solution.py:215
  25.6 8.1 %copy-start.8 = (bf16[256,256]{1,0:T(8,128)(2,1)}, bf16[256,256]{1,0:T(8,128)(2,1)S(1)}, u32[]{:S(2)}) copy-start(bf16[256,256]{1,0:T(8,128)(2,1)S(1)} %collective-permute-done.8.refs_9_) | copy-start | bytes 393220
  25.6 7.9 %collective-permute-start.10 = (bf16[256,256]{1,0:T(8,128)(2,1)S(1)}, bf16[256,256]{1,0:T(8,128)(2,1)S(1)}, u32[]{:S(2)}, u32[]{:S(2)}) collective-permute-start(bf16[256,256]{1,0:T(8,128)(2,1)S(1)} %collective-permute-done.9.refs_10_), channel_id=1, source_target_pairs={{0,1},{1,0},{2,3},{3,2},{4,5},{5,4},{6,7},{7,6},{8,9},{9,8},{10,11... | collective-permute-start | bytes 393224 | tf_op jit(solution)/shard_map/ppermute | solution.py:215
  27.9 5.8 %copy-start.9 = (bf16[256,256]{1,0:T(8,128)(2,1)}, bf16[256,256]{1,0:T(8,128)(2,1)S(1)}, u32[]{:S(2)}) copy-start(bf16[256,256]{1,0:T(8,128)(2,1)S(1)} %collective-permute-done.13.refs_14_) | copy-start | bytes 393220
  27.9 5.7 %collective-permute-start.14 = (bf16[256,256]{1,0:T(8,128)(2,1)S(1)}, bf16[256,256]{1,0:T(8,128)(2,1)S(1)}, u32[]{:S(2)}, u32[]{:S(2)}) collective-permute-start(bf16[256,256]{1,0:T(8,128)(2,1)S(1)} %collective-permute-done.13.refs_14_), channel_id=1, source_target_pairs={{0,1},{1,0},{2,3},{3,2},{4,5},{5,4},{6,7},{7,6},{8,9},{9,8},{10,11... | collective-permute-start | bytes 393224 | tf_op jit(solution)/shard_map/ppermute | solution.py:215
  33.5 0.7 %copy-start.10 = (bf16[256,256]{1,0:T(8,128)(2,1)}, bf16[256,256]{1,0:T(8,128)(2,1)S(1)}, u32[]{:S(2)}) copy-start(bf16[256,256]{1,0:T(8,128)(2,1)S(1)} %collective-permute-done.12.refs_13_) | copy-start | bytes 393220
  33.5 0.7 %copy-start.11 = (bf16[256,256]{1,0:T(8,128)(2,1)}, bf16[256,256]{1,0:T(8,128)(2,1)S(1)}, u32[]{:S(2)}) copy-start(bf16[256,256]{1,0:T(8,128)(2,1)S(1)} %collective-permute-done.2.refs_3_) | copy-start | bytes 393220
  33.5 0.7 %copy-start.12 = (bf16[256,256]{1,0:T(8,128)(2,1)}, bf16[256,256]{1,0:T(8,128)(2,1)S(1)}, u32[]{:S(2)}) copy-start(bf16[256,256]{1,0:T(8,128)(2,1)S(1)} %collective-permute-done.6.refs_7_) | copy-start | bytes 393220
  33.6 0.7 %copy-start.13 = (bf16[256,256]{1,0:T(8,128)(2,1)}, bf16[256,256]{1,0:T(8,128)(2,1)S(1)}, u32[]{:S(2)}) copy-start(bf16[256,256]{1,0:T(8,128)(2,1)S(1)} %collective-permute-done.10.refs_11_) | copy-start | bytes 393220
  33.6 0.8 %copy-start.14 = (bf16[256,256]{1,0:T(8,128)(2,1)}, bf16[256,256]{1,0:T(8,128)(2,1)S(1)}, u32[]{:S(2)}) copy-start(bf16[256,256]{1,0:T(8,128)(2,1)S(1)} %collective-permute-done.14.refs_15_) | copy-start | bytes 393220
  46.3 8.5 %collective-permute-start.15 = (bf16[256,256]{1,0:T(8,128)(2,1)}, bf16[256,256]{1,0:T(8,128)(2,1)S(1)}, u32[]{:S(2)}, u32[]{:S(2)}) collective-permute-start(bf16[256,256]{1,0:T(8,128)(2,1)} %get-tuple-element.22), channel_id=1, source_target_pairs={{0,4},{1,5},{2,6},{3,7},{4,0},{5,1},{6,2},{7,3},{8,12},{9,13},{10,... | collective-permute-start | bytes 393224 | tf_op jit(solution)/shard_map/ppermute | solution.py:215
  47.4 13.1 %collective-permute-start.16 = (bf16[256,256]{1,0:T(8,128)(2,1)}, bf16[256,256]{1,0:T(8,128)(2,1)S(1)}, u32[]{:S(2)}, u32[]{:S(2)}) collective-permute-start(bf16[256,256]{1,0:T(8,128)(2,1)} %get-tuple-element.23), channel_id=1, source_target_pairs={{0,8},{1,9},{2,10},{3,11},{4,12},{5,13},{6,14},{7,15},{8,0},{9,1},... | collective-permute-start | bytes 393224 | tf_op jit(solution)/shard_map/ppermute | solution.py:215
  49.2 11.4 %collective-permute-start.17 = (bf16[256,256]{1,0:T(8,128)(2,1)}, bf16[256,256]{1,0:T(8,128)(2,1)S(1)}, u32[]{:S(2)}, u32[]{:S(2)}) collective-permute-start(bf16[256,256]{1,0:T(8,128)(2,1)} %get-tuple-element.24), channel_id=1, source_target_pairs={{0,12},{1,13},{2,14},{3,15},{4,8},{5,9},{6,10},{7,11},{8,4},{9,5},... | collective-permute-start | bytes 393224 | tf_op jit(solution)/shard_map/ppermute | solution.py:215
  54.8 5.7 %copy-start.15 = (bf16[256,256]{1,0:T(8,128)(2,1)}, bf16[256,256]{1,0:T(8,128)(2,1)S(1)}, u32[]{:S(2)}) copy-start(bf16[256,256]{1,0:T(8,128)(2,1)S(1)} %collective-permute-done.15.refs_1_) | copy-start | bytes 393220
  60.5 0.6 %copy-start.16 = (bf16[256,256]{1,0:T(8,128)(2,1)}, bf16[256,256]{1,0:T(8,128)(2,1)S(1)}, u32[]{:S(2)}) copy-start(bf16[256,256]{1,0:T(8,128)(2,1)S(1)} %collective-permute-done.16.refs_2_) | copy-start | bytes 393220
  60.5 0.7 %copy-start.17 = (bf16[256,256]{1,0:T(8,128)(2,1)}, bf16[256,256]{1,0:T(8,128)(2,1)S(1)}, u32[]{:S(2)}) copy-start(bf16[256,256]{1,0:T(8,128)(2,1)S(1)} %collective-permute-done.17.refs_3_) | copy-start | bytes 393220

commit v2 on v1

--- a/solution.py
+++ b/solution.py
@@ -40,7 +40,7 @@
         functools.partial(whiten_kernel, spread),
         in_specs=[SMEM, ANY],
         out_specs=[VMEM] * count,
-        out_shape=[jax.ShapeDtypeStruct((own, 2 * windows), BF16)] * count,
+        out_shape=[pltpu.VMEM((own, 2 * windows), BF16)] * count,
         scratch_shapes=[
             pltpu.VMEM((count, 2, own, windows), F32),
             pltpu.SemaphoreType.DMA((count,)),
@@ -59,53 +59,18 @@
     return ((me // spread) ^ slot) * spread + ((me % spread) ^ held)
 
 
-def plan_kernel(layout, mask_s, mask_v, after, weights, subset):
-    count, spread, own, spacing, grp = layout
-    per = own // grp
-    groups = mask_v.shape[0]
-    table = mask_v[...].astype(F32).astype(BF16)
-    rowg = (lax.broadcasted_iota(jnp.int32, (2 * NTGT, groups), 0) % NTGT) * spacing // grp
-    rowpick = (rowg == lax.broadcasted_iota(jnp.int32, rowg.shape, 1)).astype(F32).astype(BF16)
-    by_target = jnp.dot(rowpick, table, preferred_element_type=F32).astype(BF16)
-
-    def block_body(at, carry):
-        first_group = source_row(spread, at // spread, at % spread) * per
-        lanes = first_group + lax.broadcasted_iota(jnp.int32, (groups, own), 1) // grp
-        onehot = (lanes == lax.broadcasted_iota(jnp.int32, (groups, own), 0)).astype(F32).astype(BF16)
-        weights[at] = jnp.dot(by_target, onehot, preferred_element_type=F32).astype(BF16)
-        for slot in range(count):
-            for part in range(per):
-                group = source_row(spread, slot, 0) * per + part
-                bits = mask_s[group, first_group]
-                for b in range(1, per):
-                    bits = bits + mask_s[group, first_group + b] * (1 << b)
-                subset[at, slot * per + part] = bits
-        return carry
-
-    lax.fori_loop(0, count * spread, block_body, 0)
-
-
-def plan(mask, after, layout):
-    count, spread, own, spacing, grp = layout
-    return pl.pallas_call(
-        functools.partial(plan_kernel, layout),
-        in_specs=[SMEM, VMEM, ANY],
-        out_specs=[VMEM, SMEM],
-        out_shape=[
-            jax.ShapeDtypeStruct((count * spread, 2 * NTGT, own), BF16),
-            jax.ShapeDtypeStruct((count * spread, count * own // grp), jnp.int32),
-        ],
-        name="plan",
-    )(mask, mask, after)
-
-
-def third_kernel(layout, subset, weights, *refs):
+def third_kernel(layout, mask_s, mask_v, *refs):
     count, spread, own, spacing, grp = layout
     blocks = refs[: count * spread]
     outs = refs[count * spread : count * spread + count]
-    everyone, trows, both, tables, moved = refs[count * spread + count :]
+    everyone, trows, both, wanted, tables, moved = refs[count * spread + count :]
     per, width, tper = own // grp, everyone.shape[-1], own // spacing
-    half = width // 2
+    half, groups, tile = width // 2, mask_v.shape[0], 16
+    rowg = (lax.broadcasted_iota(jnp.int32, (2 * NTGT, groups), 0) % NTGT) * spacing // grp
+    rowpick = (rowg == lax.broadcasted_iota(jnp.int32, rowg.shape, 1)).astype(F32).astype(BF16)
+    wanted[...] = jnp.dot(
+        rowpick, mask_v[...].astype(F32).astype(BF16), preferred_element_type=F32
+    ).astype(BF16)
     for held in range(spread):
         for slot in range(count):
             block = blocks[slot * spread + held]
@@ -121,26 +86,49 @@
         tables[slot, 0] = jnp.zeros(tables.shape[2:], F32)
     lane = lax.broadcasted_iota(jnp.int32, (1, own), 1) // grp
     only = [jnp.where(lane == part, 1.0, 0.0).astype(BF16) for part in range(per)]
+    group_rows = lax.broadcasted_iota(jnp.int32, (groups, own), 0)
+    group_lanes = lax.broadcasted_iota(jnp.int32, (groups, own), 1) // grp
 
     def held_body(held, carry):
         for slot in range(count):
             block = everyone[held * count + slot]
-            at = slot * spread + held
+            first_group = source_row(spread, slot, held) * per
+            onehot = (group_rows == first_group + group_lanes).astype(F32).astype(BF16)
+            weight = jnp.dot(wanted[...], onehot, preferred_element_type=F32)
             corr = lax.dot_general(both[...], block, NT_DIMS, preferred_element_type=F32)
-            corr = corr.astype(BF16) * weights[at]
-            for part in range(per):
-                v = jnp.dot(corr * only[part], block, preferred_element_type=F32)
-                real = v[:NTGT, :half] - v[NTGT:, half:]
-                imag = -(v[NTGT:, :half] + v[:NTGT, half:])
-                one = jnp.concatenate([real, imag], axis=1)
-                tables[slot, 1 << part] = one
-                for low in range(1, 1 << part):
-                    tables[slot, (1 << part) + low] = tables[slot, low] + one
+            corr = (corr * weight).astype(BF16)
+            parts = [corr * only[part] for part in range(per)]
+            left = jnp.concatenate(
+                [
+                    piece
+                    for t in range(0, NTGT, tile)
+                    for part in parts
+                    for piece in (part[t : t + tile], part[NTGT + t : NTGT + t + tile])
+                ],
+                axis=0,
+            )
+            v = jnp.dot(left, block, preferred_element_type=F32)
+            for t in range(0, NTGT, tile):
+                sums = [None]
+                for part in range(per):
+                    at = (t * per + part * tile) * 2
+                    vr, vi = v[at : at + tile], v[at + tile : at + 2 * tile]
+                    one = jnp.concatenate(
+                        [vr[:, :half] - vi[:, half:], -(vi[:, :half] + vr[:, half:])], axis=1
+                    )
+                    sums += [one] + [low + one for low in sums[1:]]
+                for pick in range(1, len(sums)):
+                    tables[slot, pick, t : t + tile] = sums[pick]
         for group in range(count * per):
-            total = tables[0, subset[held, group]]
-            for slot in range(1, count):
-                total = total + tables[slot, subset[slot * spread + held, group]]
-            moved[group] += total
+            receiver = source_row(spread, group // per, 0) * per + group % per
+            total = moved[group]
+            for slot in range(count):
+                first_group = source_row(spread, slot, held) * per
+                bits = mask_s[receiver, first_group]
+                for b in range(1, per):
+                    bits = bits + mask_s[receiver, first_group + b] * (1 << b)
+                total = total + tables[slot, bits]
+            moved[group] = total
         return carry
 
     lax.fori_loop(0, spread, held_body, 0)
@@ -158,7 +146,11 @@
             outs[slot][pl.ds(part * grp, grp), :] = (result * (1.0 / (half * half))).astype(BF16)
 
 
-def third(blocks, subset, weights, layout):
+def near(value):
+    return pltpu.with_memory_space_constraint(value, pltpu.VMEM)
+
+
+def third(blocks, mask, layout):
     count, spread, own, spacing, grp = layout
     width = blocks[0].shape[-1]
     per = own // grp
@@ -166,16 +158,17 @@
         functools.partial(third_kernel, layout),
         in_specs=[SMEM, VMEM] + [VMEM] * (count * spread),
         out_specs=[VMEM] * count,
-        out_shape=[jax.ShapeDtypeStruct((own, 2 * NTGT), BF16)] * count,
+        out_shape=[pltpu.VMEM((own, 2 * NTGT), BF16)] * count,
         scratch_shapes=[
             pltpu.VMEM((spread * count, own, width), BF16),
             pltpu.VMEM((NTGT, width), F32),
             pltpu.VMEM((2 * NTGT, width), BF16),
+            pltpu.VMEM((2 * NTGT, mask.shape[0]), BF16),
             pltpu.VMEM((count, 1 << per, NTGT, width), F32),
             pltpu.VMEM((count * per, NTGT, width), F32),
         ],
         name="third",
-    )(subset, weights, *blocks)
+    )(mask, mask, *map(near, blocks))
 
 
 def finish_kernel(spread, *refs):
@@ -200,7 +193,7 @@
         out_specs=VMEM,
         out_shape=jax.ShapeDtypeStruct((own * 2 * count, NTGT), F32),
         name="finish",
-    )(*blocks)
+    )(*map(near, blocks))
     return out.reshape(own, 2, count, NTGT)
 
 
@@ -215,7 +208,6 @@
         return lax.ppermute(value, "row", [(r, r ^ bits) for r in range(rows)])
 
     white = whiten(spectra, coda_bins, spread)
-    weights, subset = plan(source_mask, white[0], layout)
     blocks = [[white[0]] + [None] * (spread - 1)]
     for slot in range(1, count):
         blocks.append([swap(white[slot], slot * spread)] + [None] * (spread - 1))
@@ -226,7 +218,7 @@
                 blocks[slot][held + bit] = swap(blocks[slot][held], bit)
         bit //= 2
     flat = [blocks[slot][held] for slot in range(count) for held in range(spread)]
-    parts = third(flat, subset, weights, layout)
+    parts = third(flat, source_mask, layout)
     back = [parts[0]] + [swap(parts[slot], slot * spread) for slot in range(1, count)]
     return finish(back, spread)
 

time: 63.9 us -> 53.5 us (0.84)
  Pallas kernels: 22.8 us -> 13.2 us
  local copies, waits for them, and re-layouts: 1.41 us -> 0 us
  waiting for transfers between devices: 22.3 us -> 23.1 us
    pallas_call x1 -> x0, Pallas kernels: 5.62 us -> none  [plan(): pl.pallas_call(functools.partial(plan_kernel, layout), in_specs=[SMEM, VM...]
    pallas_call x1, Pallas kernels: 12 us -> 9.71 us  [third(): pl.pallas_call(functools.partial(third_kernel, layout), in_specs=[SMEM, V...]
    unnamed x36 -> x0, local copies, waits for them, and re-layouts: 1.41 us -> none
    pallas_call x1, Pallas kernels: 2.34 us -> 1.25 us  [finish(): pl.pallas_call(functools.partial(finish_kernel, spread), in_specs=[VMEM]...]
    ppermute x18, waiting for transfers between devices: 22.3 us -> 23.1 us  [swap(): return lax.ppermute(value, 'row', [(r, r ^ bits) for r in range(rows)])]
    pallas_call x1, Pallas kernels: 2.9 us -> 2.24 us  [whiten(): pl.pallas_call(functools.partial(whiten_kernel, spread), in_specs=[SMEM,...]
  transfers between devices with their start and end apart: 18 -> 18, of which waited for: 6 -> 7; matrix products, arithmetic and copies ran while one was open for 0% -> 0% of each run, Pallas kernels for 9% -> 0%
where the time goes in v2:
time: 53.5 us; the launch traced here: 53.3 us
  waiting for transfers between devices  23.1 us (43%)
  starting transfers between devices  16.9 us (32%)
  Pallas kernels  13.2 us (25%)
    ppermute x18, waiting for transfers between devices, swap(): return lax.ppermute(value, 'row', [(r, r ^ bits) for r in range(rows)])  23.1 us
    ppermute x18, starting transfers between devices, swap(): return lax.ppermute(value, 'row', [(r, r ^ bits) for r in range(rows)])  16.9 us
    pallas_call x1, Pallas kernels, third(): pl.pallas_call(functools.partial(third_kernel, layout), in_specs=[SMEM, V...  9.71 us
    pallas_call x1, Pallas kernels, whiten(): pl.pallas_call(functools.partial(whiten_kernel, spread), in_specs=[SMEM,...  2.24 us
    pallas_call x1, Pallas kernels, finish(): pl.pallas_call(functools.partial(finish_kernel, spread), in_specs=[VMEM]...  1.25 us
  transfers between devices with their start and end apart: 18, of which 7 were waited for; matrix products, arithmetic and copies ran while one was open for 0% of the time, Pallas kernels for 0%

profile of v2, /device:TPU:0, one launch (start us, length us, event | category | flops | bytes accessed | tf_op | source)
XLA Modules:
  0.0 53.3 jit_solution(18417675883095588582)
XLA Ops:
  0.0 2.2 %whiten.1 = (bf16[256,256]{1,0:T(8,128)(2,1)S(1)}, bf16[256,256]{1,0:T(8,128)(2,1)S(1)}, bf16[256,256]{1,0:T(8,128)(2,1)S(1)}, bf16[256,256]{1,0:T(8,128)(2,1)S(1)}) custom-call(s32[4]{0:T(128)} %bins.1, f32[2,16,256,128]{3,2,1,0:T(8,128)} %spectra.1), custom_call_target="tpu_custom_call" | custom-call | tf_op jit(solution)/shard_map/whiten/pallas_call | solution.py:39
  2.3 3.1 %collective-permute-start.3 = (bf16[256,256]{1,0:T(8,128)(2,1)S(1)}, bf16[256,256]{1,0:T(8,128)(2,1)S(1)}, u32[]{:S(2)}, u32[]{:S(2)}) collective-permute-start(bf16[256,256]{1,0:T(8,128)(2,1)S(1)} %get-tuple-element.14), channel_id=1, source_target_pairs={{0,4},{1,5},{2,6},{3,7},{4,0},{5,1},{6,2},{7,3},{8,12},{9,13},{10,... | collective-permute-start | bytes 393224 | tf_op jit(solution)/shard_map/ppermute | solution.py:208
  5.4 2.6 %collective-permute-start.7 = (bf16[256,256]{1,0:T(8,128)(2,1)S(1)}, bf16[256,256]{1,0:T(8,128)(2,1)S(1)}, u32[]{:S(2)}, u32[]{:S(2)}) collective-permute-start(bf16[256,256]{1,0:T(8,128)(2,1)S(1)} %get-tuple-element.15), channel_id=1, source_target_pairs={{0,8},{1,9},{2,10},{3,11},{4,12},{5,13},{6,14},{7,15},{8,0},{9,1},... | collective-permute-start | bytes 393224 | tf_op jit(solution)/shard_map/ppermute | solution.py:208
  8.0 0.0 collective-permute-start.11
  8.0 1.7 %collective-permute-start.1 = (bf16[256,256]{1,0:T(8,128)(2,1)S(1)}, bf16[256,256]{1,0:T(8,128)(2,1)S(1)}, u32[]{:S(2)}, u32[]{:S(2)}) collective-permute-start(bf16[256,256]{1,0:T(8,128)(2,1)S(1)} %get-tuple-element.13.refs_0_), channel_id=1, source_target_pairs={{0,2},{1,3},{2,0},{3,1},{4,6},{5,7},{6,4},{7,5},{8,10},{9,11},{10,... | collective-permute-start | bytes 393224 | tf_op jit(solution)/shard_map/ppermute | solution.py:208
  9.7 0.0 collective-permute-start
  9.7 0.7 %collective-permute-done.3.refs_4_ = bf16[256,256]{1,0:T(8,128)(2,1)S(1)} collective-permute-done((bf16[256,256]{1,0:T(8,128)(2,1)S(1)}, bf16[256,256]{1,0:T(8,128)(2,1)S(1)}, u32[]{:S(2)}, u32[]{:S(2)}) %collective-permute-start.3) | collective-permute-done | bytes 131104 | tf_op jit(solution)/shard_map/ppermute | solution.py:208
  10.4 1.7 %collective-permute-start.5 = (bf16[256,256]{1,0:T(8,128)(2,1)S(1)}, bf16[256,256]{1,0:T(8,128)(2,1)S(1)}, u32[]{:S(2)}, u32[]{:S(2)}) collective-permute-start(bf16[256,256]{1,0:T(8,128)(2,1)S(1)} %collective-permute-done.3.refs_4_), channel_id=1, source_target_pairs={{0,2},{1,3},{2,0},{3,1},{4,6},{5,7},{6,4},{7,5},{8,10},{9,11},{10,... | collective-permute-start | bytes 393224 | tf_op jit(solution)/shard_map/ppermute | solution.py:208
  12.2 6.1 %collective-permute-done.7.refs_8_ = bf16[256,256]{1,0:T(8,128)(2,1)S(1)} collective-permute-done((bf16[256,256]{1,0:T(8,128)(2,1)S(1)}, bf16[256,256]{1,0:T(8,128)(2,1)S(1)}, u32[]{:S(2)}, u32[]{:S(2)}) %collective-permute-start.7) | collective-permute-done | bytes 131104 | tf_op jit(solution)/shard_map/ppermute | solution.py:208
  18.3 0.0 collective-permute-start.4
  18.3 0.0 collective-permute-done.11.refs_12_
  18.3 1.5 %collective-permute-start.9 = (bf16[256,256]{1,0:T(8,128)(2,1)S(1)}, bf16[256,256]{1,0:T(8,128)(2,1)S(1)}, u32[]{:S(2)}, u32[]{:S(2)}) collective-permute-start(bf16[256,256]{1,0:T(8,128)(2,1)S(1)} %collective-permute-done.7.refs_8_), channel_id=1, source_target_pairs={{0,2},{1,3},{2,0},{3,1},{4,6},{5,7},{6,4},{7,5},{8,10},{9,11},{10,... | collective-permute-start | bytes 393224 | tf_op jit(solution)/shard_map/ppermute | solution.py:208
  19.8 0.0 collective-permute-done.1.refs_2_
  19.8 0.2 collective-permute-start.8
  20.0 0.0 collective-permute-done.refs_1_
  20.0 0.5 collective-permute-start.13
  20.5 0.0 collective-permute-done.5.refs_6_
  20.5 0.0 collective-permute-start.12
  20.5 0.0 collective-permute-done.4.refs_5_
  20.5 0.5 collective-permute-start.2
  21.0 3.6 %collective-permute-done.9.refs_10_ = bf16[256,256]{1,0:T(8,128)(2,1)S(1)} collective-permute-done((bf16[256,256]{1,0:T(8,128)(2,1)S(1)}, bf16[256,256]{1,0:T(8,128)(2,1)S(1)}, u32[]{:S(2)}, u32[]{:S(2)}) %collective-permute-start.9) | collective-permute-done | bytes 131104 | tf_op jit(solution)/shard_map/ppermute | solution.py:208
  24.6 0.0 collective-permute-start.6
  24.6 0.0 collective-permute-done.8.refs_9_
  24.6 0.5 collective-permute-start.10
  25.1 1.8 %collective-permute-done.13.refs_14_ = bf16[256,256]{1,0:T(8,128)(2,1)S(1)} collective-permute-done((bf16[256,256]{1,0:T(8,128)(2,1)S(1)}, bf16[256,256]{1,0:T(8,128)(2,1)S(1)}, u32[]{:S(2)}, u32[]{:S(2)}) %collective-permute-start.13) | collective-permute-done | bytes 131104 | tf_op jit(solution)/shard_map/ppermute | solution.py:208
  27.0 0.0 collective-permute-start.14
  27.0 0.0 collective-permute-done.12.refs_13_
  27.0 0.0 collective-permute-done.2.refs_3_
  27.0 0.0 collective-permute-done.6.refs_7_
  27.0 0.0 collective-permute-done.10.refs_11_
  27.0 1.3 %collective-permute-done.14.refs_15_ = bf16[256,256]{1,0:T(8,128)(2,1)S(1)} collective-permute-done((bf16[256,256]{1,0:T(8,128)(2,1)S(1)}, bf16[256,256]{1,0:T(8,128)(2,1)S(1)}, u32[]{:S(2)}, u32[]{:S(2)}) %collective-permute-start.14) | collective-permute-done | bytes 131104 | tf_op jit(solution)/shard_map/ppermute | solution.py:208
  28.3 9.7 %third.1 = (bf16[256,256]{1,0:T(8,128)(2,1)S(1)}, bf16[256,256]{1,0:T(8,128)(2,1)S(1)}, bf16[256,256]{1,0:T(8,128)(2,1)S(1)}, bf16[256,256]{1,0:T(8,128)(2,1)S(1)}) custom-call(s32[64,64]{1,0:T(8,128)} %mask_v.1, s32[64,64]{1,0:T(8,128)} %mask_v.1, bf16[256,256]{1,0:T(8,128)(2,1)S(1)} %get-tuple-element.13.refs_0_, ...), custom_call_target="tpu_custom_call" | custom-call | tf_op jit(solution)/shard_map/third/pallas_call | solution.py:157
  38.0 1.1 %collective-permute-start.15 = (bf16[256,256]{1,0:T(8,128)(2,1)S(1)}, bf16[256,256]{1,0:T(8,128)(2,1)S(1)}, u32[]{:S(2)}, u32[]{:S(2)}) collective-permute-start(bf16[256,256]{1,0:T(8,128)(2,1)S(1)} %get-tuple-element.18), channel_id=1, source_target_pairs={{0,4},{1,5},{2,6},{3,7},{4,0},{5,1},{6,2},{7,3},{8,12},{9,13},{10,... | collective-permute-start | bytes 393224 | tf_op jit(solution)/shard_map/ppermute | solution.py:208
  39.2 1.8 %collective-permute-start.16 = (bf16[256,256]{1,0:T(8,128)(2,1)S(1)}, bf16[256,256]{1,0:T(8,128)(2,1)S(1)}, u32[]{:S(2)}, u32[]{:S(2)}) collective-permute-start(bf16[256,256]{1,0:T(8,128)(2,1)S(1)} %get-tuple-element.19), channel_id=1, source_target_pairs={{0,8},{1,9},{2,10},{3,11},{4,12},{5,13},{6,14},{7,15},{8,0},{9,1},... | collective-permute-start | bytes 393224 | tf_op jit(solution)/shard_map/ppermute | solution.py:208
  40.9 1.5 %collective-permute-start.17 = (bf16[256,256]{1,0:T(8,128)(2,1)S(1)}, bf16[256,256]{1,0:T(8,128)(2,1)S(1)}, u32[]{:S(2)}, u32[]{:S(2)}) collective-permute-start(bf16[256,256]{1,0:T(8,128)(2,1)S(1)} %get-tuple-element.20), channel_id=1, source_target_pairs={{0,12},{1,13},{2,14},{3,15},{4,8},{5,9},{6,10},{7,11},{8,4},{9,5},... | collective-permute-start | bytes 393224 | tf_op jit(solution)/shard_map/ppermute | solution.py:208
  42.5 3.3 %collective-permute-done.15.refs_1_ = bf16[256,256]{1,0:T(8,128)(2,1)S(1)} collective-permute-done((bf16[256,256]{1,0:T(8,128)(2,1)S(1)}, bf16[256,256]{1,0:T(8,128)(2,1)S(1)}, u32[]{:S(2)}, u32[]{:S(2)}) %collective-permute-start.15) | collective-permute-done | bytes 131104 | tf_op jit(solution)/shard_map/ppermute | solution.py:208
  45.8 6.3 %collective-permute-done.16.refs_2_ = bf16[256,256]{1,0:T(8,128)(2,1)S(1)} collective-permute-done((bf16[256,256]{1,0:T(8,128)(2,1)S(1)}, bf16[256,256]{1,0:T(8,128)(2,1)S(1)}, u32[]{:S(2)}, u32[]{:S(2)}) %collective-permute-start.16) | collective-permute-done | bytes 131104 | tf_op jit(solution)/shard_map/ppermute | solution.py:208
  52.1 0.0 collective-permute-done.17.refs_3_
  52.1 1.3 %finish.1 = f32[2048,128]{1,0:T(8,128)} custom-call(bf16[256,256]{1,0:T(8,128)(2,1)S(1)} %get-tuple-element.17.refs_0_, bf16[256,256]{1,0:T(8,128)(2,1)S(1)} %collective-permute-done.15.refs_1_, bf16[256,256]{1,0:T(8,128)(2,1)S(1)} %collective-permute-done.16.refs_2_, bf16[256,256]{1,0:T(8,128)(2,1)S(1)} %collective-permute-done.17.refs_3_), custom_call_target="tpu_custom_call" | custom-call | tf_op jit(solution)/shard_map/finish/pallas_call | solution.py:190
Async XLA Ops:
  2.3 8.2 %collective-permute-start.3 = (bf16[256,256]{1,0:T(8,128)(2,1)S(1)}, bf16[256,256]{1,0:T(8,128)(2,1)S(1)}, u32[]{:S(2)}, u32[]{:S(2)}) collective-permute-start(bf16[256,256]{1,0:T(8,128)(2,1)S(1)} %get-tuple-element.14), channel_id=1, source_target_pairs={{0,4},{1,5},{2,6},{3,7},{4,0},{5,1},{6,2},{7,3},{8,12},{9,13},{10,... | collective-permute-start | bytes 393224 | tf_op jit(solution)/shard_map/ppermute | solution.py:208
  5.4 12.9 %collective-permute-start.7 = (bf16[256,256]{1,0:T(8,128)(2,1)S(1)}, bf16[256,256]{1,0:T(8,128)(2,1)S(1)}, u32[]{:S(2)}, u32[]{:S(2)}) collective-permute-start(bf16[256,256]{1,0:T(8,128)(2,1)S(1)} %get-tuple-element.15), channel_id=1, source_target_pairs={{0,8},{1,9},{2,10},{3,11},{4,12},{5,13},{6,14},{7,15},{8,0},{9,1},... | collective-permute-start | bytes 393224 | tf_op jit(solution)/shard_map/ppermute | solution.py:208
  8.0 10.3 %collective-permute-start.11 = (bf16[256,256]{1,0:T(8,128)(2,1)S(1)}, bf16[256,256]{1,0:T(8,128)(2,1)S(1)}, u32[]{:S(2)}, u32[]{:S(2)}) collective-permute-start(bf16[256,256]{1,0:T(8,128)(2,1)S(1)} %get-tuple-element.16), channel_id=1, source_target_pairs={{0,12},{1,13},{2,14},{3,15},{4,8},{5,9},{6,10},{7,11},{8,4},{9,5},... | collective-permute-start | bytes 393224 | tf_op jit(solution)/shard_map/ppermute | solution.py:208
  8.0 11.8 %collective-permute-start.1 = (bf16[256,256]{1,0:T(8,128)(2,1)S(1)}, bf16[256,256]{1,0:T(8,128)(2,1)S(1)}, u32[]{:S(2)}, u32[]{:S(2)}) collective-permute-start(bf16[256,256]{1,0:T(8,128)(2,1)S(1)} %get-tuple-element.13.refs_0_), channel_id=1, source_target_pairs={{0,2},{1,3},{2,0},{3,1},{4,6},{5,7},{6,4},{7,5},{8,10},{9,11},{10,... | collective-permute-start | bytes 393224 | tf_op jit(solution)/shard_map/ppermute | solution.py:208
  9.7 10.3 %collective-permute-start = (bf16[256,256]{1,0:T(8,128)(2,1)S(1)}, bf16[256,256]{1,0:T(8,128)(2,1)S(1)}, u32[]{:S(2)}, u32[]{:S(2)}) collective-permute-start(bf16[256,256]{1,0:T(8,128)(2,1)S(1)} %get-tuple-element.13.refs_0_), channel_id=1, source_target_pairs={{0,1},{1,0},{2,3},{3,2},{4,5},{5,4},{6,7},{7,6},{8,9},{9,8},{10,11... | collective-permute-start | bytes 393224 | tf_op jit(solution)/shard_map/ppermute | solution.py:208
  10.4 10.1 %collective-permute-start.5 = (bf16[256,256]{1,0:T(8,128)(2,1)S(1)}, bf16[256,256]{1,0:T(8,128)(2,1)S(1)}, u32[]{:S(2)}, u32[]{:S(2)}) collective-permute-start(bf16[256,256]{1,0:T(8,128)(2,1)S(1)} %collective-permute-done.3.refs_4_), channel_id=1, source_target_pairs={{0,2},{1,3},{2,0},{3,1},{4,6},{5,7},{6,4},{7,5},{8,10},{9,11},{10,... | collective-permute-start | bytes 393224 | tf_op jit(solution)/shard_map/ppermute | solution.py:208
  18.3 2.3 %collective-permute-start.4 = (bf16[256,256]{1,0:T(8,128)(2,1)S(1)}, bf16[256,256]{1,0:T(8,128)(2,1)S(1)}, u32[]{:S(2)}, u32[]{:S(2)}) collective-permute-start(bf16[256,256]{1,0:T(8,128)(2,1)S(1)} %collective-permute-done.3.refs_4_), channel_id=1, source_target_pairs={{0,1},{1,0},{2,3},{3,2},{4,5},{5,4},{6,7},{7,6},{8,9},{9,8},{10,11... | collective-permute-start | bytes 393224 | tf_op jit(solution)/shard_map/ppermute | solution.py:208
  18.3 6.4 %collective-permute-start.9 = (bf16[256,256]{1,0:T(8,128)(2,1)S(1)}, bf16[256,256]{1,0:T(8,128)(2,1)S(1)}, u32[]{:S(2)}, u32[]{:S(2)}) collective-permute-start(bf16[256,256]{1,0:T(8,128)(2,1)S(1)} %collective-permute-done.7.refs_8_), channel_id=1, source_target_pairs={{0,2},{1,3},{2,0},{3,1},{4,6},{5,7},{6,4},{7,5},{8,10},{9,11},{10,... | collective-permute-start | bytes 393224 | tf_op jit(solution)/shard_map/ppermute | solution.py:208
  19.8 4.9 %collective-permute-start.8 = (bf16[256,256]{1,0:T(8,128)(2,1)S(1)}, bf16[256,256]{1,0:T(8,128)(2,1)S(1)}, u32[]{:S(2)}, u32[]{:S(2)}) collective-permute-start(bf16[256,256]{1,0:T(8,128)(2,1)S(1)} %collective-permute-done.7.refs_8_), channel_id=1, source_target_pairs={{0,1},{1,0},{2,3},{3,2},{4,5},{5,4},{6,7},{7,6},{8,9},{9,8},{10,11... | collective-permute-start | bytes 393224 | tf_op jit(solution)/shard_map/ppermute | solution.py:208
  20.0 7.0 %collective-permute-start.13 = (bf16[256,256]{1,0:T(8,128)(2,1)S(1)}, bf16[256,256]{1,0:T(8,128)(2,1)S(1)}, u32[]{:S(2)}, u32[]{:S(2)}) collective-permute-start(bf16[256,256]{1,0:T(8,128)(2,1)S(1)} %collective-permute-done.11.refs_12_), channel_id=1, source_target_pairs={{0,2},{1,3},{2,0},{3,1},{4,6},{5,7},{6,4},{7,5},{8,10},{9,11},{10,... | collective-permute-start | bytes 393224 | tf_op jit(solution)/shard_map/ppermute | solution.py:208
  20.5 6.5 %collective-permute-start.12 = (bf16[256,256]{1,0:T(8,128)(2,1)S(1)}, bf16[256,256]{1,0:T(8,128)(2,1)S(1)}, u32[]{:S(2)}, u32[]{:S(2)}) collective-permute-start(bf16[256,256]{1,0:T(8,128)(2,1)S(1)} %collective-permute-done.11.refs_12_), channel_id=1, source_target_pairs={{0,1},{1,0},{2,3},{3,2},{4,5},{5,4},{6,7},{7,6},{8,9},{9,8},{10,11... | collective-permute-start | bytes 393224 | tf_op jit(solution)/shard_map/ppermute | solution.py:208
  20.5 6.5 %collective-permute-start.2 = (bf16[256,256]{1,0:T(8,128)(2,1)S(1)}, bf16[256,256]{1,0:T(8,128)(2,1)S(1)}, u32[]{:S(2)}, u32[]{:S(2)}) collective-permute-start(bf16[256,256]{1,0:T(8,128)(2,1)S(1)} %collective-permute-done.1.refs_2_), channel_id=1, source_target_pairs={{0,1},{1,0},{2,3},{3,2},{4,5},{5,4},{6,7},{7,6},{8,9},{9,8},{10,11... | collective-permute-start | bytes 393224 | tf_op jit(solution)/shard_map/ppermute | solution.py:208
  24.6 2.4 %collective-permute-start.6 = (bf16[256,256]{1,0:T(8,128)(2,1)S(1)}, bf16[256,256]{1,0:T(8,128)(2,1)S(1)}, u32[]{:S(2)}, u32[]{:S(2)}) collective-permute-start(bf16[256,256]{1,0:T(8,128)(2,1)S(1)} %collective-permute-done.5.refs_6_), channel_id=1, source_target_pairs={{0,1},{1,0},{2,3},{3,2},{4,5},{5,4},{6,7},{7,6},{8,9},{9,8},{10,11... | collective-permute-start | bytes 393224 | tf_op jit(solution)/shard_map/ppermute | solution.py:208
  24.6 2.4 %collective-permute-start.10 = (bf16[256,256]{1,0:T(8,128)(2,1)S(1)}, bf16[256,256]{1,0:T(8,128)(2,1)S(1)}, u32[]{:S(2)}, u32[]{:S(2)}) collective-permute-start(bf16[256,256]{1,0:T(8,128)(2,1)S(1)} %collective-permute-done.9.refs_10_), channel_id=1, source_target_pairs={{0,1},{1,0},{2,3},{3,2},{4,5},{5,4},{6,7},{7,6},{8,9},{9,8},{10,11... | collective-permute-start | bytes 393224 | tf_op jit(solution)/shard_map/ppermute | solution.py:208
  27.0 1.3 %collective-permute-start.14 = (bf16[256,256]{1,0:T(8,128)(2,1)S(1)}, bf16[256,256]{1,0:T(8,128)(2,1)S(1)}, u32[]{:S(2)}, u32[]{:S(2)}) collective-permute-start(bf16[256,256]{1,0:T(8,128)(2,1)S(1)} %collective-permute-done.13.refs_14_), channel_id=1, source_target_pairs={{0,1},{1,0},{2,3},{3,2},{4,5},{5,4},{6,7},{7,6},{8,9},{9,8},{10,11... | collective-permute-start | bytes 393224 | tf_op jit(solution)/shard_map/ppermute | solution.py:208
  38.0 7.7 %collective-permute-start.15 = (bf16[256,256]{1,0:T(8,128)(2,1)S(1)}, bf16[256,256]{1,0:T(8,128)(2,1)S(1)}, u32[]{:S(2)}, u32[]{:S(2)}) collective-permute-start(bf16[256,256]{1,0:T(8,128)(2,1)S(1)} %get-tuple-element.18), channel_id=1, source_target_pairs={{0,4},{1,5},{2,6},{3,7},{4,0},{5,1},{6,2},{7,3},{8,12},{9,13},{10,... | collective-permute-start | bytes 393224 | tf_op jit(solution)/shard_map/ppermute | solution.py:208
  39.2 12.9 %collective-permute-start.16 = (bf16[256,256]{1,0:T(8,128)(2,1)S(1)}, bf16[256,256]{1,0:T(8,128)(2,1)S(1)}, u32[]{:S(2)}, u32[]{:S(2)}) collective-permute-start(bf16[256,256]{1,0:T(8,128)(2,1)S(1)} %get-tuple-element.19), channel_id=1, source_target_pairs={{0,8},{1,9},{2,10},{3,11},{4,12},{5,13},{6,14},{7,15},{8,0},{9,1},... | collective-permute-start | bytes 393224 | tf_op jit(solution)/shard_map/ppermute | solution.py:208
  40.9 11.1 %collective-permute-start.17 = (bf16[256,256]{1,0:T(8,128)(2,1)S(1)}, bf16[256,256]{1,0:T(8,128)(2,1)S(1)}, u32[]{:S(2)}, u32[]{:S(2)}) collective-permute-start(bf16[256,256]{1,0:T(8,128)(2,1)S(1)} %get-tuple-element.20), channel_id=1, source_target_pairs={{0,12},{1,13},{2,14},{3,15},{4,8},{5,9},{6,10},{7,11},{8,4},{9,5},... | collective-permute-start | bytes 393224 | tf_op jit(solution)/shard_map/ppermute | solution.py:208
